TPU v7x, 128 devices: a whole 4x4x4 slice. The times are simulated.
128 devices in a mesh: seq: 32 (over z, x, core), mp: 4 (over y).
Axes of the slice: x: 4, y: 4, z: 4, core: 2. Of those that a mesh axis runs over, the one named last changes fastest.
Arguments:
- scan_points: bfloat16 [65536, 512], P('seq'), may hold values from -6 to 6
- send_order: int32 [65536], P('seq'), may hold values from 0 to 2047, as said below
- arrive_order: int32 [65536], P('seq'), may hold values from 0 to 2047, as said below
- qkv_weight: bfloat16 [512, 3, 512], P(None, None, 'mp')
- out_weight: bfloat16 [512, 512], P(None, 'mp'), may hold values from -0.25 to 0.25
- voxel_grads: bfloat16 [65536, 512], P('seq'), may hold values from -6 to 6
- voxel_shard: int32 [65536, 1], P('seq'), may hold values from 0 to 31; in each aligned block of 2048 rows (0 to 2047, 2048 to 4095, ...) at most 128 rows name the same one
- voxel_point: int32 [65536], P('seq'), may hold values from 0 to 2047
Outputs:
- d_points: float32 [65536, 512], P('seq', 'mp')
- grad_qkv: float32 [512, 3, 512], P('seq', None, 'mp')
- grad_out: float32 [512, 512], P('seq', 'mp')
Inputs may be any that keep to these rules, and one draw needn't show every extreme that they name: `send_order`: each aligned block of 2048 entries is a permutation of the numbers 0 to 2047. `arrive_order`: each aligned block of 2048 entries is a permutation of the numbers 0 to 2047. `voxel_shard`: among the rows of one device, at most 128 name the same shard.
All inputs are finite; a program needn't handle non-finite values.
Results may differ from a plain program's by a relative error of at most 0.035.
The roundings to bfloat16 on the way count: a program that leaves them out, or rounds other values in their place, can miss the bound.
Values may be sent and summed in bfloat16 or wider, within the bound.
A program may use at most 192 MiB of HBM per device.

v0:
```python
import jax
import jax.numpy as jnp
from jax import lax
from jax.sharding import PartitionSpec as P

HD = 16
PATCH = 1024


score_scale = 0.25
epsilon = 1e-05


def patch_pass(queries, key_rows, values, d_attended):
    row_count = queries.shape[0]
    head_count = queries.shape[1] // HD
    query_heads = queries.reshape(row_count, head_count, HD)
    key_heads = key_rows.reshape(row_count, head_count, HD)
    value_heads = values.reshape(row_count, head_count, HD)
    scores = (
        jnp.einsum("qhc,khc->hqk", query_heads, key_heads, preferred_element_type=jnp.float32)
        * score_scale
    )
    row_max = jnp.max(scores, axis=2, keepdims=True)
    weights_exp = jnp.exp(scores - row_max)
    probabilities = weights_exp / jnp.sum(weights_exp, axis=2, keepdims=True)
    prob_rounded = probabilities.astype(jnp.bfloat16)
    attended = jnp.einsum(
        "hqk,khc->qhc", prob_rounded, value_heads, preferred_element_type=jnp.float32
    ).astype(jnp.bfloat16)
    grad_heads = d_attended.reshape(row_count, head_count, HD)
    d_probabilities = jnp.einsum(
        "qhc,khc->hqk", grad_heads, value_heads, preferred_element_type=jnp.float32
    )
    d_values = jnp.einsum(
        "hqk,qhc->khc", prob_rounded, grad_heads, preferred_element_type=jnp.float32
    ).astype(jnp.bfloat16)
    row_delta = jnp.sum(grad_heads.astype(jnp.float32) * attended.astype(jnp.float32), axis=2)
    d_scores = (probabilities * (d_probabilities - row_delta.T[:, :, None]) * score_scale).astype(
        jnp.bfloat16
    )
    d_query = jnp.einsum(
        "hqk,khc->qhc", d_scores, key_heads, preferred_element_type=jnp.float32
    ).astype(jnp.bfloat16)
    d_keys = jnp.einsum(
        "hqk,qhc->khc", d_scores, query_heads, preferred_element_type=jnp.float32
    ).astype(jnp.bfloat16)
    stacked = jnp.stack([d_query, d_keys, d_values], axis=1).reshape(row_count, 3, head_count * HD)
    return (attended.reshape(row_count, head_count * HD), stacked)


def local(
    scan_points,
    send_order,
    arrive_order,
    qkv_weight,
    out_weight,
    voxel_grads,
    voxel_shard,
    voxel_point,
):
    shards = lax.axis_size("seq")
    local_rows = scan_points.shape[0]
    feature_count = scan_points.shape[1]
    local_cols = out_weight.shape[1]
    offset = lax.axis_index("mp") * local_cols
    outgoing = jnp.take(scan_points, send_order, axis=0)
    arrived = lax.all_to_all(outgoing, "seq", split_axis=0, concat_axis=0, tiled=True)
    points = jnp.take(arrived, arrive_order, axis=0)
    point_float = points.astype(jnp.float32)
    row_mean = jnp.mean(point_float, axis=1, keepdims=True)
    centered = point_float - row_mean
    row_var = jnp.mean(centered * centered, axis=1, keepdims=True)
    inv_scale = lax.rsqrt(row_var + epsilon)
    normed = centered * inv_scale
    hidden = normed.astype(jnp.bfloat16)
    projected = jnp.einsum(
        "pd,dtc->ptc", hidden, qkv_weight, preferred_element_type=jnp.float32
    ).astype(jnp.bfloat16)
    voxels = voxel_grads.shape[0]
    capacity = 2 * voxels // shards
    targets = voxel_shard[:, 0]
    onehot = (targets[:, None] == jnp.arange(shards, dtype=jnp.int32)[None, :]).astype(jnp.int32)
    before = jnp.cumsum(onehot, axis=0) - onehot
    places = targets * capacity + jnp.sum(before * onehot, axis=1)
    send_index = jnp.full((shards * capacity,), local_rows, jnp.int32).at[places].set(voxel_point)
    send_rows = (
        jnp.zeros((shards * capacity, feature_count), jnp.bfloat16).at[places].set(voxel_grads)
    )
    got_rows, got_index = (
        lax.all_to_all(send_rows, "seq", split_axis=0, concat_axis=0, tiled=True),
        lax.all_to_all(send_index, "seq", split_axis=0, concat_axis=0, tiled=True),
    )
    d_sum = jax.ops.segment_sum(
        got_rows.astype(jnp.float32), got_index, num_segments=local_rows + 1
    )[:local_rows]
    d_out = d_sum.astype(jnp.bfloat16)
    d_attended = jnp.dot(d_out, out_weight, preferred_element_type=jnp.float32).astype(jnp.bfloat16)
    patches = local_rows // PATCH

    def one_patch(operands):
        proj_patch, grad_patch = operands
        return patch_pass(proj_patch[:, 0], proj_patch[:, 1], proj_patch[:, 2], grad_patch)

    attended, d_projected = lax.map(
        one_patch,
        (
            projected.reshape(patches, PATCH, 3, local_cols),
            d_attended.reshape(patches, PATCH, local_cols),
        ),
    )
    attended = attended.reshape(local_rows, local_cols)
    d_projected = d_projected.reshape(local_rows, 3, local_cols)
    upper = jnp.einsum("pd,ptc->dtc", hidden, d_projected, preferred_element_type=jnp.float32)
    lower = jnp.dot(d_out.T, attended, preferred_element_type=jnp.float32)
    summed = lax.psum_scatter(
        jnp.concatenate([upper, lower[:, None, :]], axis=1).astype(jnp.bfloat16),
        "seq",
        scatter_dimension=0,
        tiled=True,
    ).astype(jnp.float32)
    grad_qkv = summed[:, :3, :]
    grad_out = summed[:, 3, :]
    d_partial = jnp.einsum(
        "ptc,dtc->pd", d_projected, qkv_weight, preferred_element_type=jnp.float32
    )
    d_hidden = lax.psum(d_partial.astype(jnp.bfloat16), "mp").astype(jnp.float32)
    mean_grad = jnp.mean(d_hidden, axis=1, keepdims=True)
    mean_cross = jnp.mean(d_hidden * normed, axis=1, keepdims=True)
    full_grad = d_out.astype(jnp.float32) + inv_scale * (d_hidden - mean_grad - normed * mean_cross)
    d_points = lax.dynamic_slice_in_dim(full_grad, offset, local_cols, 1)
    return (d_points, grad_qkv, grad_out)


def solution(mesh):
    in_specs = (
        P("seq", None),
        P("seq"),
        P("seq"),
        P(None, None, "mp"),
        P(None, "mp"),
        P("seq", None),
        P("seq", None),
        P("seq"),
    )
    out_specs = (P("seq", "mp"), P("seq", None, "mp"), P("seq", "mp"))
    return jax.shard_map(local, mesh=mesh, in_specs=in_specs, out_specs=out_specs, check_vma=False)
```

profile of v0, /device:TPU:1, one launch (start us, length us, event | category | flops | bytes accessed | tf_op | source)
XLA Modules:
  0.0 459.8 jit_solution(11573179876489189796)
XLA Ops:
  8.0 0.9 fusion.32
  8.9 9.1 %reduce-window.6 = s32[32,16,128]{2,1,0:T(8,128)S(1)} reduce-window(s32[32,16,128]{2,1,0:T(8,128)S(1)} %fusion.32, s32[]{:T(128)} %constant.33.clone.1), window={size=1x1x128 pad=0_0x0_0x127_0}, to_apply=%region_0.1 | reduce-window | flops 8323072 | bytes 524292 | tf_op jit(solution)/shard_map/reduce-window
  18.7 0.8 fusion.31
  20.2 8.8 %scatter_custom_fusion = s32[4096]{0:T(1024)} fusion(s32[2048]{0:T(1024)S(1)} %bitcast.166, s32[2048]{0:T(1024)} %param.19, s32[]{:T(128)} %constant.31.clone.1), kind=kCustom, calls=%fused_computation.70 | custom fusion | bytes 16896 | tf_op jit(solution)/shard_map/scatter | solution.py:86
  29.0 9.4 %all-to-all-start = ((s32[32,128,1]{1,2,0:T(1,128)}), s32[32,128,1]{1,2,0:T(1,128)S(1)}, u32[]{:S(2)}, u32[]{:S(2)}) async-start(s32[32,128,1]{1,2,0:T(1,128)} %bitcast.22), calls=%async_computation | async-start | bytes 32768 | tf_op jit(solution)/shard_map/all_to_all | solution.py:92
  39.9 9.2 %gather_fusion = bf16[2048,512]{1,0:T(8,128)(2,1)} fusion(bf16[2048,512]{1,0:T(8,128)(2,1)S(1)} %copy-done, s32[2048]{0:T(1024)S(1)} %fusion.35), kind=kCustom, calls=%fused_computation.clone | custom fusion | bytes 4202496 | tf_op jit(solution)/shard_map/jit(_take)/gather | solution.py:67
  49.0 2.8 broadcast_select_fusion.1
  51.8 7.4 %all-to-all-start.2 = ((bf16[32,64,512]{2,1,0:T(8,128)(2,1)}), bf16[32,64,512]{2,1,0:T(8,128)(2,1)S(1)}, u32[]{:S(2)}, u32[]{:S(2)}) async-start(bf16[32,64,512]{2,1,0:T(8,128)(2,1)} %bitcast.155), calls=%async_computation.2 | async-start | bytes 4194304 | tf_op jit(solution)/shard_map/all_to_all | solution.py:68
  59.2 12.6 %scatter_custom_fusion.1 = bf16[4096,512]{1,0:T(8,128)(2,1)} fusion(s32[2048]{0:T(1024)S(1)} %bitcast.167, bf16[2048,512]{1,0:T(8,128)(2,1)} %param.17, bf16[]{:T(256)} %constant.28.clone.1), kind=kCustom, calls=%fused_computation.42 | custom fusion | bytes 4194816 | tf_op jit(solution)/shard_map/scatter | solution.py:88
  71.8 15.2 %all-to-all-done.2 = bf16[32,64,512]{2,1,0:T(8,128)(2,1)S(1)} async-done(((bf16[32,64,512]{2,1,0:T(8,128)(2,1)}), bf16[32,64,512]{2,1,0:T(8,128)(2,1)S(1)}, u32[]{:S(2)}, u32[]{:S(2)}) %all-to-all-start.2) | async-done | bytes 2097184 | tf_op jit(solution)/shard_map/all_to_all | solution.py:68
  87.0 6.9 %all-to-all-start.1 = ((bf16[32,128,512]{2,1,0:T(8,128)(2,1)}), bf16[32,128,512]{2,1,0:T(8,128)(2,1)}, u32[]{:S(2)}, u32[]{:S(2)}) async-start(bf16[32,128,512]{2,1,0:T(8,128)(2,1)} %bitcast.153), calls=%async_computation.1 | async-start | bytes 8388608 | tf_op jit(solution)/shard_map/all_to_all | solution.py:91
  94.5 9.2 %gather_fusion.1 = bf16[2048,512]{1,0:T(8,128)(2,1)} fusion(bf16[2048,512]{1,0:T(8,128)(2,1)S(1)} %bitcast.138, s32[2048]{0:T(1024)S(1)} %fusion.36), kind=kCustom, calls=%fused_computation.1.clone | custom fusion | bytes 4202496 | tf_op jit(solution)/shard_map/jit(_take)/gather | solution.py:69
  103.7 2.2 convert_reduce_fusion
  106.0 2.7 fusion.13
  109.3 3.3 convolution_convert_fusion.4
  112.6 31.7 %all-to-all-done.1 = bf16[32,128,512]{2,1,0:T(8,128)(2,1)} async-done(((bf16[32,128,512]{2,1,0:T(8,128)(2,1)}), bf16[32,128,512]{2,1,0:T(8,128)(2,1)}, u32[]{:S(2)}, u32[]{:S(2)}) %all-to-all-start.1) | async-done | bytes 4194336 | tf_op jit(solution)/shard_map/all_to_all | solution.py:91
  144.4 30.5 %scatter_custom_fusion.2 = f32[2049,512]{1,0:T(8,128)} fusion(s32[4096]{0:T(1024)S(1)} %bitcast.165, bf16[4096,512]{1,0:T(8,128)(2,1)} %bitcast.42, f32[]{:T(128)} %constant.30.clone.1), kind=kCustom, calls=%fused_computation.25 | custom fusion | flops 4194304 | bytes 8390660 | tf_op jit(solution)/shard_map/scatter-add | solution.py:94
  174.9 2.9 convolution_convert_fusion.5
  177.8 182.6 %while.12 = (s32[]{:T(128)}, bf16[2,1024,128]{2,1,0:T(8,128)(2,1)S(1)}, bf16[2,1024,3,128]{3,1,0,2:T(8,128)(2,1)}, bf16[2,1024,3,128]{3,1,0,2:T(8,128)(2,1)}, bf16[2,1024,128]{2,1,0:T(8,128)(2,1)S(1)}, /*index=5*/s32[]{:T(128)}) while((s32[]{:T(128)}, bf16[2,1024,128]{2,1,0:T(8,128)(2,1)S(1)}, bf16[2,1024,3,128]{3,1,0,2:T(8,128)(2,1)}, ...), condition=%wide.region_12.14_spmd, body=%wide.region_8.13_spmd.sunk | while | flops 1696326656 | bytes 283541632 | solution.py:105
  189.9 1.2 constant_dynamic-slice_fusion.5
  191.4 14.6 %fusion.91 = (f32[8,1024]{1,0:T(8,128)S(1)}, f32[8,1024,1024]{1,2,0:T(8,128)}) fusion(bf16[1024,8,16]{0,2,1:T(8,128)(2,1)S(1)} %bitcast.144, bf16[1024,8,16]{0,2,1:T(8,128)(2,1)S(1)} %bitcast.146), kind=kOutput, calls=%fused_computation.80.clone.1 | convolution fusion | flops 293602304 | bytes 34111488 | tf_op jit(solution)/shard_map/while/body/eval_jaxpr/sub | solution.py:25
  206.0 17.8 %fusion.92 = bf16[8,1024,1024]{1,2,0:T(8,128)(2,1)} fusion(f32[8,1024,1024]{1,2,0:T(8,128)} %get-tuple-element.112, f32[8,1024]{1,0:T(8,128)S(1)} %get-tuple-element.113), kind=kLoop, calls=%fused_computation.12.clone.1 | loop fusion | flops 16777216 | bytes 50364416 | tf_op jit(solution)/shard_map/while/body/eval_jaxpr/convert_element_type | solution.py:27
  223.8 10.2 %convolution_convert_fusion.10 = bf16[8,16,1024]{2,1,0:T(8,128)(2,1)S(1)} fusion(bf16[1024,8,16]{0,2,1:T(8,128)(2,1)S(1)} %bitcast.140, bf16[8,1024,1024]{1,2,0:T(8,128)(2,1)} %fusion.92), kind=kOutput, calls=%fused_computation.14.clone.1 | convolution fusion | flops 268566528 | bytes 17301504 | tf_op jit(solution)/shard_map/while/body/eval_jaxpr/hqk,qhc->khc/dot_general | solution.py:35
  234.0 8.1 %multiply_reduce_fusion.4 = (f32[1024,8]{0,1:T(8,128)S(1)}, bf16[8,16,1024]{2,1,0:T(8,128)(2,1)S(1)}) fusion(bf16[1024,8,16]{0,2,1:T(8,128)(2,1)S(1)} %bitcast.141, bf16[1024,8,16]{0,2,1:T(8,128)(2,1)S(1)} %bitcast.148, bf16[8,1024,1024]{1,2,0:T(8,128)(2,1)} %fusion.92), kind=kOutput, calls=%fused_computation.19.clone.1 | convolution fusion | flops 269082624 | bytes 17596416 | tf_op jit(solution)/shard_map/while/body/eval_jaxpr/hqk,khc->qhc/dot_general | solution.py:28
  242.2 13.0 %multiply_convert_fusion.2 = bf16[8,1024,1024]{1,2,0:T(8,128)(2,1)S(1)} fusion(f32[8,1024]{1,0:T(8,128)S(1)} %bitcast.158, f32[8,1024,1024]{1,2,0:T(8,128)} %get-tuple-element.112, f32[8,1024]{1,0:T(8,128)S(1)} %get-tuple-element.113, bf16[1024,8,16]{0,2,1:T(8,128)(2,1)S(1)} %bitcast.142, bf16[1024,8,16]{0,2,1:T(8,128)(2,1)S(1)} %bitcast.149), kind=kOutput, calls=%fused_computation.6.clone.1 | convolution fusion | flops 310378496 | bytes 50921472 | tf_op jit(solution)/shard_map/while/body/eval_jaxpr/qhc,khc->hqk/dot_general | solution.py:32
  255.2 5.7 %copy-done.2 = bf16[8,1024,1024]{1,2,0:T(8,128)(2,1)} copy-done((bf16[8,1024,1024]{1,2,0:T(8,128)(2,1)}, bf16[8,1024,1024]{1,2,0:T(8,128)(2,1)S(1)}, u32[]{:S(2)}) %copy-start.2) | copy-done | bytes 16777240 | tf_op jit(solution)/shard_map/while
  260.9 2.3 convolution_convert_fusion.12
  263.2 10.2 %convolution_convert_fusion.11 = bf16[8,16,1024]{2,1,0:T(8,128)(2,1)S(1)} fusion(bf16[1024,8,16]{0,2,1:T(8,128)(2,1)S(1)} %bitcast.145, bf16[8,1024,1024]{1,2,0:T(8,128)(2,1)} %copy-done.2), kind=kOutput, calls=%fused_computation.15.clone.1 | convolution fusion | flops 268566528 | bytes 17301504 | tf_op jit(solution)/shard_map/while/body/eval_jaxpr/hqk,qhc->khc/dot_general | solution.py:45
  274.0 1.1 constant_dynamic-update-slice_fusion.5
  275.2 1.2 constant_dynamic-slice_fusion.5
  276.8 14.5 %fusion.91 = (f32[8,1024]{1,0:T(8,128)S(1)}, f32[8,1024,1024]{1,2,0:T(8,128)}) fusion(bf16[1024,8,16]{0,2,1:T(8,128)(2,1)S(1)} %bitcast.144, bf16[1024,8,16]{0,2,1:T(8,128)(2,1)S(1)} %bitcast.146), kind=kOutput, calls=%fused_computation.80.clone.1 | convolution fusion | flops 293602304 | bytes 34111488 | tf_op jit(solution)/shard_map/while/body/eval_jaxpr/sub | solution.py:25
  291.3 17.8 %fusion.92 = bf16[8,1024,1024]{1,2,0:T(8,128)(2,1)} fusion(f32[8,1024,1024]{1,2,0:T(8,128)} %get-tuple-element.112, f32[8,1024]{1,0:T(8,128)S(1)} %get-tuple-element.113), kind=kLoop, calls=%fused_computation.12.clone.1 | loop fusion | flops 16777216 | bytes 50364416 | tf_op jit(solution)/shard_map/while/body/eval_jaxpr/convert_element_type | solution.py:27
  309.1 10.2 %convolution_convert_fusion.10 = bf16[8,16,1024]{2,1,0:T(8,128)(2,1)S(1)} fusion(bf16[1024,8,16]{0,2,1:T(8,128)(2,1)S(1)} %bitcast.140, bf16[8,1024,1024]{1,2,0:T(8,128)(2,1)} %fusion.92), kind=kOutput, calls=%fused_computation.14.clone.1 | convolution fusion | flops 268566528 | bytes 17301504 | tf_op jit(solution)/shard_map/while/body/eval_jaxpr/hqk,qhc->khc/dot_general | solution.py:35
  319.3 8.1 %multiply_reduce_fusion.4 = (f32[1024,8]{0,1:T(8,128)S(1)}, bf16[8,16,1024]{2,1,0:T(8,128)(2,1)S(1)}) fusion(bf16[1024,8,16]{0,2,1:T(8,128)(2,1)S(1)} %bitcast.141, bf16[1024,8,16]{0,2,1:T(8,128)(2,1)S(1)} %bitcast.148, bf16[8,1024,1024]{1,2,0:T(8,128)(2,1)} %fusion.92), kind=kOutput, calls=%fused_computation.19.clone.1 | convolution fusion | flops 269082624 | bytes 17596416 | tf_op jit(solution)/shard_map/while/body/eval_jaxpr/hqk,khc->qhc/dot_general | solution.py:28
  327.6 13.0 %multiply_convert_fusion.2 = bf16[8,1024,1024]{1,2,0:T(8,128)(2,1)S(1)} fusion(f32[8,1024]{1,0:T(8,128)S(1)} %bitcast.158, f32[8,1024,1024]{1,2,0:T(8,128)} %get-tuple-element.112, f32[8,1024]{1,0:T(8,128)S(1)} %get-tuple-element.113, bf16[1024,8,16]{0,2,1:T(8,128)(2,1)S(1)} %bitcast.142, bf16[1024,8,16]{0,2,1:T(8,128)(2,1)S(1)} %bitcast.149), kind=kOutput, calls=%fused_computation.6.clone.1 | convolution fusion | flops 310378496 | bytes 50921472 | tf_op jit(solution)/shard_map/while/body/eval_jaxpr/qhc,khc->hqk/dot_general | solution.py:32
  340.6 5.7 %copy-done.2 = bf16[8,1024,1024]{1,2,0:T(8,128)(2,1)} copy-done((bf16[8,1024,1024]{1,2,0:T(8,128)(2,1)}, bf16[8,1024,1024]{1,2,0:T(8,128)(2,1)S(1)}, u32[]{:S(2)}) %copy-start.2) | copy-done | bytes 16777240 | tf_op jit(solution)/shard_map/while
  346.3 2.3 convolution_convert_fusion.12
  348.6 10.2 %convolution_convert_fusion.11 = bf16[8,16,1024]{2,1,0:T(8,128)(2,1)S(1)} fusion(bf16[1024,8,16]{0,2,1:T(8,128)(2,1)S(1)} %bitcast.145, bf16[8,1024,1024]{1,2,0:T(8,128)(2,1)} %copy-done.2), kind=kOutput, calls=%fused_computation.15.clone.1 | convolution fusion | flops 268566528 | bytes 17301504 | tf_op jit(solution)/shard_map/while/body/eval_jaxpr/hqk,qhc->khc/dot_general | solution.py:45
  359.4 1.0 constant_dynamic-update-slice_fusion.5
  360.4 3.1 fusion.23
  363.8 2.2 fusion.20
  366.0 0.8 pad_maximum_fusion.1
  366.9 4.0 bitcast_convert_fusion
  371.0 3.8 slice.44
  374.8 67.1 %reduce-scatter.2.cloned.1.call-done = bf16[16,4,128]{2,0,1:T(8,128)(2,1)} async-done(((bf16[512,4,128]{2,0,1:T(8,128)(2,1)}), bf16[16,4,128]{2,0,1:T(8,128)(2,1)}) %reduce-scatter.2.cloned.1.call-update) | async-done | bytes 16400 | tf_op jit(solution)/shard_map/reduce_scatter | solution.py:116
  441.9 1.3 slice.40
  444.5 4.2 convert_reduce_fusion.1
  449.4 2.7 fusion.26
  (73 shorter events, 8.5 us)
Async XLA Ops:
  8.0 31.9 %copy-start = (bf16[2048,512]{1,0:T(8,128)(2,1)S(1)}, bf16[2048,512]{1,0:T(8,128)(2,1)}, u32[]{:S(2)}) copy-start(bf16[2048,512]{1,0:T(8,128)(2,1)} %param.12) | copy-start | bytes 6291460
  29.0 22.8 %all-to-all-start = ((s32[32,128,1]{1,2,0:T(1,128)}), s32[32,128,1]{1,2,0:T(1,128)S(1)}, u32[]{:S(2)}, u32[]{:S(2)}) async-start(s32[32,128,1]{1,2,0:T(1,128)} %bitcast.22), calls=%async_computation | async-start | bytes 32768 | tf_op jit(solution)/shard_map/all_to_all | solution.py:92
  51.8 35.2 %all-to-all-start.2 = ((bf16[32,64,512]{2,1,0:T(8,128)(2,1)}), bf16[32,64,512]{2,1,0:T(8,128)(2,1)S(1)}, u32[]{:S(2)}, u32[]{:S(2)}) async-start(bf16[32,64,512]{2,1,0:T(8,128)(2,1)} %bitcast.155), calls=%async_computation.2 | async-start | bytes 4194304 | tf_op jit(solution)/shard_map/all_to_all | solution.py:68
  87.0 7.4 %copy-start.13 = (s32[2048]{0:T(1024)S(1)}, s32[2048]{0:T(1024)}, u32[]{:S(2)}) copy-start(s32[2048]{0:T(1024)} %param.14) | copy-start | bytes 24580
  87.0 57.3 %all-to-all-start.1 = ((bf16[32,128,512]{2,1,0:T(8,128)(2,1)}), bf16[32,128,512]{2,1,0:T(8,128)(2,1)}, u32[]{:S(2)}, u32[]{:S(2)}) async-start(bf16[32,128,512]{2,1,0:T(8,128)(2,1)} %bitcast.153), calls=%async_computation.1 | async-start | bytes 8388608 | tf_op jit(solution)/shard_map/all_to_all | solution.py:91
  94.0 347.9 %reduce-scatter.2.cloned.1.call-start = ((), (), s32[]{:S(2)}) async-start(), calls=%async_computation.5 | async-start | bytes 540672 | tf_op jit(solution)/shard_map/reduce_scatter | solution.py:116
  94.5 14.2 %copy-start.11 = (pred[2048]{0:T(1024)(128)(4,1)}, pred[2048]{0:T(1024)(128)(4,1)S(1)}, u32[]{:S(2)}) copy-start(pred[2048]{0:T(1024)(128)(4,1)S(1)} %compare_and_fusion) | copy-start | bytes 6148
  103.7 5.6 %copy-start.3 = (bf16[2048,512]{1,0:T(8,128)(2,1)S(1)}, bf16[2048,512]{1,0:T(8,128)(2,1)}, u32[]{:S(2)}) copy-start(bf16[2048,512]{1,0:T(8,128)(2,1)} %gather_fusion.1) | copy-start | bytes 6291460
  103.7 5.6 %copy-start.15 = (bf16[512,3,128]{2,0,1:T(8,128)(2,1)S(1)}, bf16[512,3,128]{2,0,1:T(8,128)(2,1)}, u32[]{:S(2)}) copy-start(bf16[512,3,128]{2,0,1:T(8,128)(2,1)} %param.15) | copy-start | bytes 1179652
  105.9 2.8 copy-start.9
  108.7 0.6 copy-start.7
  144.4 30.5 %copy-start.6 = (bf16[512,128]{1,0:T(8,128)(2,1)S(1)}, bf16[512,128]{1,0:T(8,128)(2,1)}, u32[]{:S(2)}) copy-start(bf16[512,128]{1,0:T(8,128)(2,1)} %param.16) | copy-start | bytes 393220
  255.2 5.7 %copy-start.2 = (bf16[8,1024,1024]{1,2,0:T(8,128)(2,1)}, bf16[8,1024,1024]{1,2,0:T(8,128)(2,1)S(1)}, u32[]{:S(2)}) copy-start(bf16[8,1024,1024]{1,2,0:T(8,128)(2,1)S(1)} %multiply_convert_fusion.2) | copy-start | bytes 50331652 | tf_op jit(solution)/shard_map/while
  340.6 5.7 %copy-start.2 = (bf16[8,1024,1024]{1,2,0:T(8,128)(2,1)}, bf16[8,1024,1024]{1,2,0:T(8,128)(2,1)S(1)}, u32[]{:S(2)}) copy-start(bf16[8,1024,1024]{1,2,0:T(8,128)(2,1)S(1)} %multiply_convert_fusion.2) | copy-start | bytes 50331652 | tf_op jit(solution)/shard_map/while
  360.4 3.1 copy-start.4
  360.4 3.1 copy-start.8
  360.4 3.1 copy-start.10
  360.4 3.2 copy-start.12
  360.4 3.3 copy-start.14
  363.8 3.1 copy-start.16
  366.9 77.7 %all-reduce.2.cloned.1.call-start = ((), (), s32[]{:S(2)}) async-start(), calls=%async_computation.4 | async-start | bytes 4194304 | tf_op jit(solution)/shard_map/psum | solution.py:127
  444.5 4.3 copy-start.5
  448.8 3.4 copy-start.1
Sparse Core Ops, SparseCore 0:
  367.0 74.8 reduce-scatter.1
Sparse Core Ops, SparseCore 1:
  371.1 57.7 all-reduce.1
where the time goes:
time: 468 us; the launch traced here: 460 us
  matrix products  132 us (28%)
  waiting for transfers between devices  114 us (24%)
  other arithmetic  96.4 us (21%)
  local copies, waits for them, and re-layouts  64.7 us (14%)
  starting transfers between devices  24.2 us (5%)
  between operations  16 us (3%)
  loops' own time  12 us (3%)
    reduce_scatter x1, waiting for transfers between devices, local(): lax.psum_scatter(jnp.concatenate([upper, lower[:, None, :]], axis=1).asty...  67.1 us
    convert_element_type x2, other arithmetic, patch_pass(): prob_rounded = probabilities.astype(jnp.bfloat16)  35.6 us
    all_to_all x1, waiting for transfers between devices, local(): lax.all_to_all(send_rows, 'seq', split_axis=0, concat_axis=0, tiled=True)  31.7 us
    scatter-add x1, other arithmetic, local(): jax.ops.segment_sum(got_rows.astype(jnp.float32), got_index, num_segments...  30.5 us
    sub x2, matrix products, patch_pass(): weights_exp = jnp.exp(scores - row_max)  29.1 us
    dot_general x2, matrix products, patch_pass(): jnp.einsum('qhc,khc->hqk', grad_heads, value_heads, preferred_element_typ...  26 us
    dot_general x2, matrix products, patch_pass(): jnp.einsum('hqk,qhc->khc', d_scores, query_heads, preferred_element_type=...  20.4 us
    dot_general x2, matrix products, patch_pass(): jnp.einsum('hqk,qhc->khc', prob_rounded, grad_heads, preferred_element_ty...  20.4 us
  transfers between devices with their start and end apart: 5, of which 3 were waited for; matrix products, arithmetic and copies ran while one was open for 12% of the time, Pallas kernels for 0%

commit v1 on v0

v1 whole, which is shorter than its diff:
```python
import jax
import jax.numpy as jnp
from jax import lax
from jax.experimental import pallas as pl
from jax.experimental.pallas import tpu as pltpu
from jax.sharding import PartitionSpec as P

HD = 16
PATCH = 1024
LANES = 128
BLK = 256
QB = 256
EPSILON = 1e-05
LOG2E = 1.4426950408889634
BF = jnp.bfloat16
F32 = jnp.float32
MESH = pl.DeviceIdType.MESH


def dotf(a, b):
    return jnp.dot(a, b, preferred_element_type=F32)


def dot_nt(a, b):
    return lax.dot_general(a, b, (((1,), (1,)), ((), ())), preferred_element_type=F32)


def iota(shape, axis):
    return lax.broadcasted_iota(jnp.int32, shape, axis)


def as_mask(cond):
    return jnp.where(cond, 1.0, 0.0).astype(BF)


def lane_copy(row):
    return jnp.broadcast_to(row.astype(F32), (LANES, BLK)).T


def select_rows(order_row, count):
    want = lane_copy(order_row).astype(jnp.int32)
    lane = iota((BLK, LANES), 1)
    return jnp.concatenate([as_mask(want == lane + c * LANES) for c in range(count // LANES)], axis=1)


def exchange_kernel(
    scan, voxels, send_order, arrive_order, shard, point,
    pts, dout,
    x, v, sendp, sendv, sendi, gotp, gotv, goti, place,
    in_sem, send_sem, recv_sem, ring_send, ring_recv,
):
    seq, mp = lax.axis_index("seq"), lax.axis_index("mp")
    n, m = lax.axis_size("seq"), lax.axis_size("mp")
    rows = x.shape[0]
    grp = rows // n
    cap = gotv.shape[0] // n
    blocks = rows // BLK
    right, left = lax.rem(mp + 1, m), lax.rem(mp + m - 1, m)
    mine = pl.ds(pl.multiple_of(mp * LANES, LANES), LANES)
    in_x = pltpu.make_async_copy(scan.at[:, mine], x, in_sem.at[0])
    in_v = pltpu.make_async_copy(voxels.at[:, mine], v, in_sem.at[1])
    in_x.start()
    in_v.start()
    barrier = pltpu.get_barrier_semaphore()
    for k in range(1, n):
        pl.semaphore_signal(barrier, inc=1, device_id={"seq": lax.rem(seq + k, n)}, device_id_type=MESH)
    pl.semaphore_signal(barrier, inc=1, device_id={"mp": right}, device_id_type=MESH)
    pl.semaphore_signal(barrier, inc=1, device_id={"mp": left}, device_id_type=MESH)

    tri = as_mask(iota((BLK, BLK), 0) < iota((BLK, BLK), 1))
    carry = jnp.zeros((n, 1), F32)
    codes = jnp.zeros((3 * n, cap), F32)
    for b in range(blocks):
        target = shard[b : b + 1, :]
        hot = jnp.where(iota((n, BLK), 0) == target, 1.0, 0.0)
        before = dotf(hot.astype(BF), tri) + carry
        rank = jnp.sum(before * hot, axis=0, keepdims=True)
        carry = carry + jnp.sum(hot, axis=1, keepdims=True)
        place[b : b + 1, :] = target * cap + rank.astype(jnp.int32)
        where_to = point[b : b + 1, :]
        high = (where_to // 64).astype(F32)
        low = (where_to % 64).astype(F32)
        slot = as_mask(iota((cap, BLK), 0) == rank.astype(jnp.int32))
        coded = jnp.concatenate([hot * high, hot * low, hot], axis=0).astype(BF)
        codes = codes + dot_nt(coded, slot)
    sub = iota((16, cap), 0)
    for t in range(n):
        sendi[t] = jnp.where(
            sub == 0, codes[t : t + 1], jnp.where(sub == 1, codes[n + t : n + t + 1], codes[2 * n + t : 2 * n + t + 1])
        ).astype(BF)

    pl.semaphore_wait(barrier, n + 1)

    def send(src, dst, kind, peer):
        return pltpu.make_async_remote_copy(
            src_ref=src, dst_ref=dst, send_sem=send_sem.at[kind], recv_sem=recv_sem.at[kind],
            device_id={"seq": peer}, device_id_type=MESH,
        )

    def rows_of(block, size):
        return pl.ds(pl.multiple_of(block * size, size), size)

    in_x.wait()
    per = BLK // grp

    def points_out(i, _):
        b = lax.rem(i + seq // per, blocks)
        hot = select_rows(send_order[pl.ds(b, 1), :], rows)
        sendp[rows_of(b, BLK), :] = dotf(hot, x[...]).astype(BF)
        for u in range(per):
            peer = b * per + u

            @pl.when(peer != seq)
            def _():
                send(sendp.at[rows_of(peer, grp)], gotp.at[rows_of(seq, grp)], 0, peer).start()

        return 0

    lax.fori_loop(0, blocks, points_out, 0)
    gotp[rows_of(seq, grp), :] = sendp[rows_of(seq, grp), :]
    in_v.wait()
    per_v = BLK // cap
    vblocks = n // per_v

    def voxels_out(i, _):
        b = lax.rem(i + seq // per_v, vblocks)
        slot = iota((BLK, BLK), 0) + b * BLK
        hot = jnp.concatenate([as_mask(slot == place[c : c + 1, :]) for c in range(blocks)], axis=1)
        sendv[rows_of(b, BLK), :] = dotf(hot, v[...]).astype(BF)
        for u in range(per_v):
            peer = b * per_v + u

            @pl.when(peer != seq)
            def _():
                send(sendv.at[rows_of(peer, cap)], gotv.at[rows_of(seq, cap)], 1, peer).start()
                send(sendi.at[peer], goti.at[seq], 2, peer).start()

        return 0

    lax.fori_loop(0, vblocks, voxels_out, 0)
    gotv[rows_of(seq, cap), :] = sendv[rows_of(seq, cap), :]
    goti[seq] = sendi[seq]

    def ring(full, kind, owner, b, to):
        at = full.at[owner, rows_of(b, BLK)]
        return pltpu.make_async_remote_copy(
            src_ref=at, dst_ref=at, send_sem=ring_send.at[kind], recv_sem=ring_recv.at[kind, owner, b],
            device_id={"mp": to}, device_id_type=MESH,
        )

    half = blocks // 2

    def relay(full, kind, b):
        @pl.when(b < half)
        def _():
            ring(full, kind, left, b, right).wait_recv()
            ring(full, kind, left, b, right).start()

        @pl.when(b >= half)
        def _():
            ring(full, kind, right, b, left).wait_recv()
            ring(full, kind, right, b, left).start()

    def wait_all(kind, ref, part):
        other = ref.at[pl.ds(0, part)]
        send(other, other, kind, seq).wait_recv()
        send(other, other, kind, seq).wait_send()

    wait_all(0, gotp, (n - 1) * grp)

    def points_in(b, _):
        hot = select_rows(arrive_order[pl.ds(b, 1), :], rows)
        pts[mp, rows_of(b, BLK), :] = dotf(hot, gotp[...]).astype(BF)
        ring(pts, 0, mp, b, right).start()
        ring(pts, 0, mp, b, left).start()
        return 0

    lax.fori_loop(0, blocks, points_in, 0)
    wait_all(1, gotv, (n - 1) * cap)
    wait_all(2, goti, n - 1)

    def voxels_in(b, _):
        pos = iota((BLK, cap), 0) + b * BLK
        tiles = []
        for s in range(n):
            code = goti[s].astype(F32)
            at = jnp.where(code[2:3, :] > 0.5, code[0:1, :] * 64.0 + code[1:2, :], -1.0).astype(jnp.int32)
            tiles.append(as_mask(pos == at))
        dout[mp, rows_of(b, BLK), :] = dotf(jnp.concatenate(tiles, axis=1), gotv[...]).astype(BF)
        ring(dout, 1, mp, b, right).start()
        ring(dout, 1, mp, b, left).start()
        relay(pts, 0, b)
        return 0

    lax.fori_loop(0, blocks, voxels_in, 0)

    def late(b, _):
        relay(dout, 1, b)
        return 0

    lax.fori_loop(0, blocks, late, 0)
    opposite = lax.rem(mp + 2, m)
    for kind, full in ((0, pts), (1, dout)):
        for b in range(blocks):
            ring(full, kind, left if b >= half else right, b, right).wait_recv()
            ring(full, kind, opposite, b, right).wait_recv()
        for _ in range(2):
            ring_all = full.at[0]
            pltpu.make_async_remote_copy(
                src_ref=ring_all, dst_ref=ring_all, send_sem=ring_send.at[kind], recv_sem=ring_recv.at[kind, 0, 0],
                device_id={"mp": right}, device_id_type=MESH,
            ).wait_send()
        ring_half = full.at[0]
        pltpu.make_async_remote_copy(
            src_ref=ring_half, dst_ref=ring_half, send_sem=ring_send.at[kind], recv_sem=ring_recv.at[kind, 0, 0],
            device_id={"mp": right}, device_id_type=MESH,
        ).wait_send()


def exchange(scan, voxels, send_order, arrive_order, shard, point, n, m):
    rows = scan.shape[0]
    grp, cap = rows // n, 2 * voxels.shape[0] // n
    blocks = rows // BLK
    vmem, hbm = pl.BlockSpec(memory_space=pltpu.VMEM), pl.BlockSpec(memory_space=pl.ANY)
    dma = pltpu.SemaphoreType.DMA
    return pl.pallas_call(
        exchange_kernel,
        out_shape=[jax.ShapeDtypeStruct((m, rows, LANES), BF)] * 2,
        in_specs=[hbm, hbm, vmem, vmem, vmem, vmem],
        out_specs=[vmem, vmem],
        scratch_shapes=[
            pltpu.VMEM((rows, LANES), BF),
            pltpu.VMEM((rows, LANES), BF),
            pltpu.VMEM((rows, LANES), BF),
            pltpu.VMEM((n * cap, LANES), BF),
            pltpu.VMEM((n, 16, cap), BF),
            pltpu.VMEM((rows, LANES), BF),
            pltpu.VMEM((n * cap, LANES), BF),
            pltpu.VMEM((n, 16, cap), BF),
            pltpu.VMEM((blocks, BLK), jnp.int32),
            dma((2,)),
            dma((3,)),
            dma((3,)),
            dma((2,)),
            dma((2, m, blocks)),
        ],
        compiler_params=pltpu.CompilerParams(
            collective_id=0, has_side_effects=True, vmem_limit_bytes=48 * 1024 * 1024
        ),
        name="exchange",
    )(
        scan, voxels, send_order.reshape(blocks, BLK), arrive_order.reshape(blocks, BLK),
        shard.reshape(blocks, BLK), point.reshape(blocks, BLK),
    )


def lanes_of(ref, r):
    return jnp.concatenate([ref[j, r, :] for j in range(ref.shape[0])], axis=1)


def core_kernel(
    points, dout, wq, wk, wv, wo, part, grads, stats, normq, invb,
    hid, kk, vv, qhl, qn, kt, vt, dat, dpt, qm, s_ref, e_ref, ds_ref, dan, dvk,
):
    m, rows, _ = points.shape
    npatch = rows // PATCH
    wcat = jnp.concatenate([wq[...], wk[...], wv[...]], axis=1)
    ones_lane = as_mask(iota((BLK, LANES), 1) < 3)
    for p in range(npatch):
        for b in range(PATCH // BLK):
            r = pl.ds(p * PATCH + b * BLK, BLK)
            c = pl.ds(b * BLK, BLK)
            x = lanes_of(points, r).astype(F32)
            x = x - jnp.mean(x, axis=1, keepdims=True)
            inv = lax.rsqrt(jnp.mean(x * x, axis=1, keepdims=True) + EPSILON)
            normed = x * inv
            hidden = normed.astype(BF)
            hid[r, :] = hidden
            invb[r, :] = jnp.broadcast_to(inv, (BLK, LANES))
            mp = lax.axis_index("mp")
            own = normed[:, 0:LANES]
            for j in range(1, m):
                own = jnp.where(mp == j, normed[:, j * LANES : (j + 1) * LANES], own)
            normq[r, :] = own
            proj = dotf(hidden, wcat)
            q, k, v = (proj[:, t * LANES : (t + 1) * LANES].astype(BF) for t in range(3))
            qn[r, :] = q
            kk[r, 0:LANES] = k
            kk[r, LANES : 2 * LANES] = k
            vv[r, 0:LANES] = v
            vv[r, LANES : 2 * LANES] = ones_lane
            qs = (q.astype(F32) * (0.25 * LOG2E)).T
            high = qs.astype(BF)
            qhl[p, 0:LANES, c] = high
            qhl[p, LANES : 2 * LANES, c] = (qs - high.astype(F32)).astype(BF)
            kt[p, :, c] = k.astype(F32).T.astype(BF)
            vt[p, :, c] = v.astype(F32).T.astype(BF)
            dat[p, :, c] = dotf(lanes_of(dout, r), wo[...]).astype(BF).astype(F32).T.astype(BF)

    def patch_body(p, _):
        prow = pl.ds(pl.multiple_of(p * PATCH, PATCH), PATCH)
        dvk[...] = jnp.zeros_like(dvk)

        def head_body(h, _):
            hrow = pl.ds(pl.multiple_of(h * HD, HD), HD)
            rmask = (iota((LANES, PATCH), 0) // HD) == h
            zero = jnp.zeros((LANES, PATCH), BF)
            qm[0:LANES, :] = jnp.where(rmask, qhl[p, 0:LANES, :], zero)
            qm[LANES : 2 * LANES, :] = jnp.where(rmask, qhl[p, LANES : 2 * LANES, :], zero)
            lmask = (iota((PATCH, LANES), 1) // HD) == h
            k2 = kk[prow, :]
            v2 = vv[prow, :]
            vt1 = jnp.concatenate([vt[p, hrow, :], jnp.ones((HD, PATCH), BF)], axis=0)
            kth = kt[p, hrow, :]
            for b in range(PATCH // QB):
                c = pl.ds(b * QB, QB)
                s_ref[b % 2] = dotf(k2, qm[:, c])
                top = jnp.max(s_ref[b % 2], axis=0, keepdims=True)
                e = jnp.exp2(s_ref[b % 2] - top).astype(BF)
                e_ref[:, c] = e
                av = dotf(vt1, e)
                inv = 1.0 / av[HD : HD + 1, :]
                att = (av[0:HD, :] * inv).astype(BF)
                dpt[p, pl.ds(pl.multiple_of(3 * LANES + h * HD, HD), HD), c] = att
                da = (dat[p, hrow, c].astype(F32) * inv).astype(BF).astype(F32)
                delta = jnp.sum(da * att.astype(F32), axis=0, keepdims=True)
                d1 = delta.astype(BF).astype(F32)
                d2 = (delta - d1).astype(BF).astype(F32)
                d3 = delta - d1 - d2
                sub = iota((LANES, QB), 0)
                tile = jnp.where(sub // HD == h, jnp.concatenate([da] * (LANES // HD), axis=0), 0.0)
                tail = jnp.where(sub == 0, -d1, jnp.where(sub == 1, -d2, jnp.where(sub == 2, -d3, 0.0)))
                dan[c, :] = tile.T.astype(BF)
                dp = dotf(v2, jnp.concatenate([tile, tail], axis=0).astype(BF))
                ds = (e_ref[:, c].astype(F32) * dp).astype(BF)
                ds_ref[:, c] = ds
                dpt[p, hrow, c] = (dotf(kth, ds) * 0.25).astype(BF)
            dvk[:, 0:LANES] += dotf(ds_ref[...], jnp.where(lmask, qn[prow, :], jnp.zeros((PATCH, LANES), BF)))
            dvk[:, LANES : 2 * LANES] += dotf(e_ref[...], dan[...])
            return 0

        lax.fori_loop(0, LANES // HD, head_body, 0)
        dk = (dvk[:, 0:LANES] * 0.25).astype(BF)
        dv = dvk[:, LANES : 2 * LANES].astype(BF)
        dpt[p, LANES : 2 * LANES, :] = dk.astype(F32).T.astype(BF)
        dpt[p, 2 * LANES : 3 * LANES, :] = dv.astype(F32).T.astype(BF)
        dq = dpt[p, 0:LANES, :].astype(F32).T.astype(BF)
        dproj = jnp.concatenate([dq, dk, dv], axis=1)
        for b in range(PATCH // BLK):
            r = pl.ds(pl.multiple_of(p * PATCH + b * BLK, BLK), BLK)
            pd = dot_nt(dproj[b * BLK : (b + 1) * BLK], wcat).astype(BF)
            for j in range(m):
                part[j, r, :] = pd[:, j * LANES : (j + 1) * LANES]
            x = lanes_of(points, r).astype(F32)
            normed = (x - jnp.mean(x, axis=1, keepdims=True)) * invb[r, 0:1]
            z = pd.astype(F32) * normed
            zh = z.astype(BF)
            zl = (z - zh.astype(F32)).astype(BF)
            on = jnp.ones((8, pd.shape[1]), BF)
            total = dot_nt(on, pd)
            cross = dot_nt(on, zh) + dot_nt(on, zl)
            stats[p, :, b * BLK : (b + 1) * BLK] = jnp.where(iota((8, BLK), 0) == 0, total, cross)
        return 0

    lax.fori_loop(0, npatch, patch_body, 0)
    upper, lower = 0.0, 0.0
    for p in range(npatch):
        r = pl.ds(p * PATCH, PATCH)
        upper = upper + dotf(dpt[p, 0 : 3 * LANES, :], hid[r, :])
        lower = lower + dotf(dpt[p, 3 * LANES : 4 * LANES, :], lanes_of(dout, r))
    grads[:, 0 : 3 * LANES] = upper.T.astype(BF)
    grads[:, 3 * LANES : 4 * LANES] = lower.T.astype(BF)


def core(points, dout, wq, wk, wv, wo):
    m, rows, _ = points.shape
    npatch = rows // PATCH
    feats = m * LANES
    vmem = pl.BlockSpec(memory_space=pltpu.VMEM)
    return pl.pallas_call(
        core_kernel,
        out_shape=[
            jax.ShapeDtypeStruct((m, rows, LANES), BF),
            jax.ShapeDtypeStruct((feats, 4 * LANES), BF),
            jax.ShapeDtypeStruct((npatch, 8, PATCH), F32),
            jax.ShapeDtypeStruct((rows, LANES), F32),
            jax.ShapeDtypeStruct((rows, LANES), F32),
        ],
        in_specs=[vmem] * 6,
        out_specs=[vmem] * 5,
        scratch_shapes=[
            pltpu.VMEM((rows, feats), BF),
            pltpu.VMEM((rows, 2 * LANES), BF),
            pltpu.VMEM((rows, 2 * LANES), BF),
            pltpu.VMEM((npatch, 2 * LANES, PATCH), BF),
            pltpu.VMEM((rows, LANES), BF),
            pltpu.VMEM((npatch, LANES, PATCH), BF),
            pltpu.VMEM((npatch, LANES, PATCH), BF),
            pltpu.VMEM((npatch, LANES, PATCH), BF),
            pltpu.VMEM((npatch, 4 * LANES, PATCH), BF),
            pltpu.VMEM((2 * LANES, PATCH), BF),
            pltpu.VMEM((2, PATCH, QB), F32),
            pltpu.VMEM((PATCH, PATCH), BF),
            pltpu.VMEM((PATCH, PATCH), BF),
            pltpu.VMEM((PATCH, LANES), BF),
            pltpu.VMEM((PATCH, 2 * LANES), F32),
        ],
        compiler_params=pltpu.CompilerParams(vmem_limit_bytes=60 * 1024 * 1024),
        name="core",
    )(points, dout, wq, wk, wv, wo)


def finish_kernel(
    part, grads, stats, normq, invb, dout,
    d_points, grad_qkv, grad_out,
    got_l, got_r, rel_l, rel_r, got_s, got_g,
    g_send, g_recv, s_send, s_recv, p_send, p_recv,
):
    seq, mp = lax.axis_index("seq"), lax.axis_index("mp")
    n, m = lax.axis_size("seq"), lax.axis_size("mp")
    rows = normq.shape[0]
    npatch = rows // PATCH
    right, left, opposite = lax.rem(mp + 1, m), lax.rem(mp + m - 1, m), lax.rem(mp + 2, m)
    barrier = pltpu.get_barrier_semaphore()
    for k in range(1, n):
        pl.semaphore_signal(barrier, inc=1, device_id={"seq": lax.rem(seq + k, n)}, device_id_type=MESH)
    for to in (right, left, opposite):
        pl.semaphore_signal(barrier, inc=1, device_id={"mp": to}, device_id_type=MESH)
    pl.semaphore_wait(barrier, n - 1 + m - 1)
    half = rows // 2
    low, high = pl.ds(0, half), pl.ds(half, half)

    def hop(src, dst, sem, to):
        return pltpu.make_async_remote_copy(
            src_ref=src, dst_ref=dst, send_sem=p_send.at[sem], recv_sem=p_recv.at[sem],
            device_id={"mp": to}, device_id_type=MESH,
        )

    first = [
        hop(part.at[opposite, low], rel_l, 0, right),
        hop(part.at[opposite, high], rel_r, 1, left),
        hop(part.at[right, high], got_l.at[high], 2, right),
        hop(part.at[left, low], got_r.at[low], 3, left),
    ]
    for c in first:
        c.start()

    def stat_copy(i, to):
        return pltpu.make_async_remote_copy(
            src_ref=stats, dst_ref=got_s.at[i], send_sem=s_send.at[i], recv_sem=s_recv.at[i],
            device_id={"mp": to}, device_id_type=MESH,
        )

    for i, to in enumerate((right, left, opposite)):
        stat_copy(i, to).start()
    band = grads.shape[0] // n

    def grad_copy(src, dst, peer):
        return pltpu.make_async_remote_copy(
            src_ref=src, dst_ref=dst, send_sem=g_send, recv_sem=g_recv,
            device_id={"seq": peer}, device_id_type=MESH,
        )

    def grads_out(k, _):
        peer = lax.rem(seq + k, n)
        at = pl.ds(pl.multiple_of(peer * band, band), band)
        grad_copy(grads.at[at], got_g.at[seq], peer).start()
        return 0

    lax.fori_loop(1, n, grads_out, 0)
    got_g[seq] = grads[pl.ds(pl.multiple_of(seq * band, band), band), :]
    first[0].wait_recv()
    first[0].wait_send()
    rel_l[...] = (rel_l[...].astype(F32) + part[right, low, :].astype(F32)).astype(BF)
    second_r = hop(rel_l, got_l.at[low], 4, right)
    second_r.start()
    first[1].wait_recv()
    first[1].wait_send()
    rel_r[...] = (rel_r[...].astype(F32) + part[left, high, :].astype(F32)).astype(BF)
    second_l = hop(rel_r, got_r.at[high], 5, left)
    second_l.start()
    others = got_g.at[pl.ds(0, n - 1)]
    grad_copy(others, others, seq).wait()
    total = jnp.zeros((band, grads.shape[1]), F32)
    for k in range(n):
        total = total + got_g[k].astype(F32)
    for t in range(3):
        grad_qkv[:, t, :] = total[:, t * LANES : (t + 1) * LANES]
    grad_out[...] = total[:, 3 * LANES : 4 * LANES]
    for i, to in enumerate((right, left, opposite)):
        stat_copy(i, to).wait()
    first[2].wait()
    first[3].wait()
    second_r.wait()
    second_l.wait()
    scale = 1.0 / (m * LANES)
    for p in range(npatch):
        st = (stats[p] + got_s[0, p] + got_s[1, p] + got_s[2, p]) * scale
        for b in range(PATCH // BLK):
            r = pl.ds(p * PATCH + b * BLK, BLK)
            mean_grad = lane_copy(st[0:1, b * BLK : (b + 1) * BLK])
            mean_cross = lane_copy(st[1:2, b * BLK : (b + 1) * BLK])
            d_hidden = part[mp, r, :].astype(F32) + got_l[r, :].astype(F32) + got_r[r, :].astype(F32)
            d_points[r, :] = dout[mp, r, :].astype(F32) + invb[r, :] * (
                d_hidden - mean_grad - normq[r, :] * mean_cross
            )


def finish(part, grads, stats, normq, invb, dout, n):
    m, rows, _ = part.shape
    npatch = rows // PATCH
    band = grads.shape[0] // n
    vmem = pl.BlockSpec(memory_space=pltpu.VMEM)
    dma = pltpu.SemaphoreType.DMA
    return pl.pallas_call(
        finish_kernel,
        out_shape=[
            jax.ShapeDtypeStruct((rows, LANES), F32),
            jax.ShapeDtypeStruct((band, 3, LANES), F32),
            jax.ShapeDtypeStruct((band, LANES), F32),
        ],
        in_specs=[vmem] * 6,
        out_specs=[vmem] * 3,
        scratch_shapes=[
            pltpu.VMEM((rows, LANES), BF),
            pltpu.VMEM((rows, LANES), BF),
            pltpu.VMEM((rows // 2, LANES), BF),
            pltpu.VMEM((rows // 2, LANES), BF),
            pltpu.VMEM((m - 1, npatch, 8, PATCH), F32),
            pltpu.VMEM((n, band, 4 * LANES), BF),
            dma(()),
            dma(()),
            dma((m - 1,)),
            dma((m - 1,)),
            dma((6,)),
            dma((6,)),
        ],
        compiler_params=pltpu.CompilerParams(
            collective_id=1, has_side_effects=True, vmem_limit_bytes=48 * 1024 * 1024
        ),
        name="finish",
    )(part, grads, stats, normq, invb, dout)


def local(
    scan_points, send_order, arrive_order, qkv_weight, out_weight, voxel_grads, voxel_shard, voxel_point
):
    n, m = lax.axis_size("seq"), lax.axis_size("mp")
    pts, dout = exchange(
        scan_points, voxel_grads, send_order, arrive_order, voxel_shard, voxel_point, n, m
    )
    part, grads, stats, normq, invb = core(
        pts, dout, qkv_weight[:, 0], qkv_weight[:, 1], qkv_weight[:, 2], out_weight
    )
    return tuple(finish(part, grads, stats, normq, invb, dout, n))


def solution(mesh):
    in_specs = (
        P("seq", None), P("seq"), P("seq"), P(None, None, "mp"), P(None, "mp"),
        P("seq", None), P("seq", None), P("seq"),
    )
    out_specs = (P("seq", "mp"), P("seq", None, "mp"), P("seq", "mp"))
    return jax.shard_map(local, mesh=mesh, in_specs=in_specs, out_specs=out_specs, check_vma=False)
```

time: 468 us -> 205 us (0.44); the launches traced: 460 us -> 204 us
  Pallas kernels: 0 us -> 187 us
  matrix products: 132 us -> 0 us
  waiting for transfers between devices: 114 us -> 0 us
  other arithmetic: 96.4 us -> 1.36 us
  local copies, waits for them, and re-layouts: 64.7 us -> 15.2 us
  starting transfers between devices: 24.2 us -> 0 us
  between operations: 16 us -> 0.68 us
  loops' own time: 12 us -> 0 us
    pallas_call x0 -> x3, Pallas kernels: none -> 187 us  [the longest x1 101 us: core(): pl.pallas_call(core_kernel, out_shape=[jax.ShapeDtypeStruct((m, rows, LAN...]
    dot_general x15 -> x0, matrix products: 103 us -> none  [the longest x2 26 us: patch_pass(): jnp.einsum('qhc,khc->hqk', grad_heads, value_heads, preferred_element_typ...]
    reduce_scatter x1 -> x0, waiting for transfers between devices: 67.1 us -> none  [local(): lax.psum_scatter(jnp.concatenate([upper, lower[:, None, :]], axis=1).asty...]
    all_to_all x3 -> x0, waiting for transfers between devices: 47 us -> none  [the longest x1 31.7 us: local(): lax.all_to_all(send_rows, 'seq', split_axis=0, concat_axis=0, tiled=True)]
    convert_element_type x5 -> x0, other arithmetic: 37.8 us -> none  [the longest x2 35.6 us: patch_pass(): prob_rounded = probabilities.astype(jnp.bfloat16)]
    scatter-add x1 -> x0, other arithmetic: 30.5 us -> none  [local(): jax.ops.segment_sum(got_rows.astype(jnp.float32), got_index, num_segments...]
    sub x2 -> x0, matrix products: 29.1 us -> none  [patch_pass(): weights_exp = jnp.exp(scores - row_max)]
    all_to_all x3 -> x0, starting transfers between devices: 23.8 us -> none  [the longest x1 9.43 us: local(): lax.all_to_all(send_index, 'seq', split_axis=0, concat_axis=0, tiled=True)]
  transfers between devices with their start and end apart: 5 -> 0, of which waited for: 3 -> 0; matrix products, arithmetic and copies ran while one was open for 12% -> 0% of each run, Pallas kernels for 0% -> 0%
where the time goes in v1:
time: 205 us; the launch traced here: 204 us
  Pallas kernels  187 us (91%)
  local copies, waits for them, and re-layouts  15.2 us (7%)
    pallas_call x1, Pallas kernels, core(): pl.pallas_call(core_kernel, out_shape=[jax.ShapeDtypeStruct((m, rows, LAN...  101 us
    pallas_call x1, Pallas kernels, exchange(): pl.pallas_call(exchange_kernel, out_shape=[jax.ShapeDtypeStruct((m, rows,...  58.5 us
    pallas_call x1, Pallas kernels, finish(): pl.pallas_call(finish_kernel, out_shape=[jax.ShapeDtypeStruct((rows, LANE...  27.6 us
    unnamed x17, local copies, waits for them, and re-layouts  10.6 us

profile of v1, /device:TPU:1, one launch (start us, length us, event | category | flops | bytes accessed | tf_op | source)
XLA Modules:
  0.0 204.1 jit_solution(3003875828107227038)
XLA Ops:
  0.6 0.5 broadcast.3
  1.1 1.4 reduce.3
  2.5 0.7 reshape.18.send_order
  3.2 0.7 reshape.19.arrive_order
  3.9 0.7 reshape.21.point
  4.6 1.8 slice_bitcast_fusion
  6.4 58.5 %exchange.1 = (bf16[4,2048,128]{2,1,0:T(8,128)(2,1)S(1)}, bf16[4,2048,128]{2,1,0:T(8,128)(2,1)S(1)}) custom-call(bf16[2048,512]{1,0:T(8,128)(2,1)} %scan.1, bf16[2048,512]{1,0:T(8,128)(2,1)} %voxels.1, s32[8,256]{1,0:T(8,128)S(1)} %reshape.18.send_order, s32[8,256]{1,0:T(8,128)S(1)} %reshape.19.arrive_order, s32[8,256]{1,0:T(8,128)S(1)} %reshape.20.shard, ...), custom_call_target="tpu_custom_call" | custom-call | tf_op jit(solution)/shard_map/exchange/pallas_call | solution.py:226
  65.0 0.0 copy-start
  65.0 1.3 copy-done
  66.3 0.0 copy-start.1
  66.3 1.3 copy-done.1
  67.6 100.7 %core.1 = (bf16[4,2048,128]{2,1,0:T(8,128)(2,1)}, bf16[512,512]{1,0:T(8,128)(2,1)}, f32[2,8,1024]{2,1,0:T(8,128)}, f32[2048,128]{1,0:T(8,128)}, f32[2048,128]{1,0:T(8,128)}) custom-call(bf16[4,2048,128]{2,1,0:T(8,128)(2,1)} %copy-done.1, bf16[4,2048,128]{2,1,0:T(8,128)(2,1)} %copy-done, bf16[512,128]{1,0:T(8,128)(2,1)} %get-tuple-element.21.wq, ...), custom_call_target="tpu_custom_call" | custom-call | tf_op jit(solution)/shard_map/core/pallas_call | solution.py:380
  168.4 0.0 copy-start.2
  168.4 1.6 copy-done.2
  170.0 0.0 copy-start.3
  170.0 1.2 copy-done.3
  171.2 0.0 copy-start.4
  171.2 1.2 copy-done.4
  172.4 0.0 copy-start.5
  172.4 1.0 copy-done.5
  173.5 0.0 copy-start.6
  173.5 0.8 copy-done.6
  174.3 27.6 %finish.1 = (f32[2048,128]{1,0:T(8,128)S(1)}, f32[16,3,128]{2,1,0:T(4,128)S(1)}, f32[16,128]{1,0:T(8,128)S(1)}) custom-call(bf16[4,2048,128]{2,1,0:T(8,128)(2,1)S(1)} %copy-done.2, bf16[512,512]{1,0:T(8,128)(2,1)S(1)} %copy-done.5, f32[2,8,1024]{2,1,0:T(8,128)S(1)} %copy-done.6, f32[2048,128]{1,0:T(8,128)S(1)} %copy-done.3, f32[2048,128]{1,0:T(8,128)S(1)} %copy-done.4, ...), custom_call_target="tpu_custom_call" | custom-call | tf_op jit(solution)/shard_map/finish/pallas_call | solution.py:515
  201.9 0.6 copy.11
  202.5 1.0 copy.14
  203.5 0.6 copy.15
  (1 shorter events, 0.0 us)
Async XLA Ops:
  65.0 1.3 copy-start
  66.3 1.3 copy-start.1
  168.4 1.6 copy-start.2
  170.0 1.2 copy-start.3
  171.2 1.2 copy-start.4
  172.4 1.0 copy-start.5
  173.5 0.8 copy-start.6

commit v2 on v0

v2 whole, which is shorter than its diff:
```python
import jax
import jax.numpy as jnp
from jax import lax
from jax.experimental import pallas as pl
from jax.experimental.pallas import tpu as pltpu
from jax.sharding import PartitionSpec as P

HD = 16
PATCH = 1024
LANES = 128
BLK = 256
HEADS = LANES // HD
PBLK = PATCH // BLK
QH = 512
EPSILON = 1e-05
LOG2E = 1.4426950408889634
BF = jnp.bfloat16
F32 = jnp.float32
MESH = pl.DeviceIdType.MESH


def dotf(a, b):
    return jnp.dot(a, b, preferred_element_type=F32)


def dot_nt(a, b):
    return lax.dot_general(a, b, (((1,), (1,)), ((), ())), preferred_element_type=F32)


def iota(shape, axis):
    return lax.broadcasted_iota(jnp.int32, shape, axis)


def as_mask(cond):
    return jnp.where(cond, 1.0, 0.0).astype(BF)


def lane_copy(row):
    return jnp.broadcast_to(row.astype(F32), (LANES, BLK)).T


def select_rows(order_row, count):
    want = lane_copy(order_row).astype(jnp.int32)
    lane = iota((BLK, LANES), 1)
    return jnp.concatenate([as_mask(want == lane + c * LANES) for c in range(count // LANES)], axis=1)


def lanes_of(ref, r):
    return jnp.concatenate([ref[j, r, :] for j in range(ref.shape[0])], axis=1)


def rows_of(block, size):
    return pl.ds(pl.multiple_of(block * size, size), size)


def remote(src, dst, send_sem, recv_sem, axis, to):
    return pltpu.make_async_remote_copy(
        src_ref=src, dst_ref=dst, send_sem=send_sem, recv_sem=recv_sem,
        device_id={axis: to}, device_id_type=MESH,
    )


def layer_kernel(
    scan, voxels, orders, wq, wk, wv, wo,
    d_points, grad_qkv, grad_out,
    x, v, sendp, sendv, sendi, gotp, gotv, goti, place,
    pts, dout, hid, kn, vn, qhl, qt, kt, vt, dat, dpt, qm0, qm1, s0, s1, e_all, ds0, ds1, top, linv,
    grads, stats, invb, rel_l, rel_r, got_s, got_g,
    in_sem, send_sem, recv_sem, ring_send, ring_recv, p_send, p_recv, s_send, s_recv, g_send, g_recv,
):
    seq, mp = lax.axis_index("seq"), lax.axis_index("mp")
    n, m = lax.axis_size("seq"), lax.axis_size("mp")
    rows = x.shape[0]
    npatch = rows // PATCH
    grp = rows // n
    cap = gotv.shape[0] // n
    blocks = rows // BLK
    right, left, opposite = lax.rem(mp + 1, m), lax.rem(mp + m - 1, m), lax.rem(mp + 2, m)
    part, got_l, got_r = pts, x, v
    send_order, arrive_order, shard, point = (orders.at[i] for i in range(4))

    mine = pl.ds(pl.multiple_of(mp * LANES, LANES), LANES)
    in_x = pltpu.make_async_copy(scan.at[:, mine], x, in_sem.at[0])
    in_v = pltpu.make_async_copy(voxels.at[:, mine], v, in_sem.at[1])
    in_x.start()
    in_v.start()
    barrier = pltpu.get_barrier_semaphore()
    for k in range(1, n):
        pl.semaphore_signal(barrier, inc=1, device_id={"seq": lax.rem(seq + k, n)}, device_id_type=MESH)
    for to in (right, left, opposite):
        pl.semaphore_signal(barrier, inc=1, device_id={"mp": to}, device_id_type=MESH)

    def send(src, dst, kind, peer):
        return remote(src, dst, send_sem.at[kind], recv_sem.at[kind], "seq", peer)

    in_x.wait()
    pl.semaphore_wait(barrier, n + m - 2)
    per = BLK // grp

    def points_out(i, _):
        b = lax.rem(i + seq // per, blocks)
        hot = select_rows(send_order[pl.ds(b, 1), :], rows)
        sendp[rows_of(b, BLK), :] = dotf(hot, x[...]).astype(BF)
        for u in range(per):
            peer = b * per + u

            @pl.when(peer != seq)
            def _():
                send(sendp.at[rows_of(peer, grp)], gotp.at[rows_of(seq, grp)], 0, peer).start()

        return 0

    lax.fori_loop(0, blocks, points_out, 0)
    gotp[rows_of(seq, grp), :] = sendp[rows_of(seq, grp), :]

    tri = as_mask(iota((BLK, BLK), 0) < iota((BLK, BLK), 1))
    carry = jnp.zeros((n, 1), F32)
    codes = jnp.zeros((3 * n, cap), F32)
    for b in range(blocks):
        target = shard[b : b + 1, :]
        hot = jnp.where(iota((n, BLK), 0) == target, 1.0, 0.0)
        before = dotf(hot.astype(BF), tri) + carry
        rank = jnp.sum(before * hot, axis=0, keepdims=True)
        carry = carry + jnp.sum(hot, axis=1, keepdims=True)
        place[b : b + 1, :] = target * cap + rank.astype(jnp.int32)
        where_to = point[b : b + 1, :]
        high = (where_to // 64).astype(F32)
        low = (where_to % 64).astype(F32)
        slot = as_mask(iota((cap, BLK), 0) == rank.astype(jnp.int32))
        coded = jnp.concatenate([hot * high, hot * low, hot], axis=0).astype(BF)
        codes = codes + dot_nt(coded, slot)
    sub16 = iota((16, cap), 0)
    for t in range(n):
        a, b, c = codes[t : t + 1], codes[n + t : n + t + 1], codes[2 * n + t : 2 * n + t + 1]
        sendi[t] = jnp.where(sub16 == 0, a, jnp.where(sub16 == 1, b, c)).astype(BF)
    in_v.wait()
    per_v = BLK // cap
    vblocks = n // per_v

    def voxels_out(i, _):
        b = lax.rem(i + seq // per_v, vblocks)
        slot = iota((BLK, BLK), 0) + b * BLK
        hot = jnp.concatenate([as_mask(slot == place[c : c + 1, :]) for c in range(blocks)], axis=1)
        sendv[rows_of(b, BLK), :] = dotf(hot, v[...]).astype(BF)
        for u in range(per_v):
            peer = b * per_v + u

            @pl.when(peer != seq)
            def _():
                send(sendv.at[rows_of(peer, cap)], gotv.at[rows_of(seq, cap)], 1, peer).start()
                send(sendi.at[peer], goti.at[seq], 2, peer).start()

        return 0

    def wait_all(kind, ref, size):
        other = ref.at[pl.ds(0, size)]
        send(other, other, kind, seq).wait_recv()
        send(other, other, kind, seq).wait_send()

    def ring(full, kind, owner, b, to):
        at = full.at[owner, rows_of(b, BLK)]
        return remote(at, at, ring_send.at[kind], ring_recv.at[kind, owner, b], "mp", to)

    def goes_right(b):
        return lax.rem(b, PBLK) < PBLK // 2

    def relay(full, kind, b):
        @pl.when(goes_right(b))
        def _():
            ring(full, kind, left, b, right).wait_recv()
            ring(full, kind, left, b, right).start()

        @pl.when(jnp.logical_not(goes_right(b)))
        def _():
            ring(full, kind, right, b, left).wait_recv()
            ring(full, kind, right, b, left).start()

    def arrived(full, kind, b):
        @pl.when(goes_right(b))
        def _():
            ring(full, kind, right, b, left).wait_recv()

        @pl.when(jnp.logical_not(goes_right(b)))
        def _():
            ring(full, kind, left, b, right).wait_recv()

        ring(full, kind, opposite, b, right).wait_recv()

    def ring_sent(full, kind):
        for _ in range(3):
            remote(full.at[0], full.at[0], ring_send.at[kind], ring_recv.at[kind, 0, 0], "mp", right).wait_send()

    wait_all(0, gotp, (n - 1) * grp)

    def points_in(b, _):
        hot = select_rows(arrive_order[pl.ds(b, 1), :], rows)
        pts[mp, rows_of(b, BLK), :] = dotf(hot, gotp[...]).astype(BF)
        ring(pts, 0, mp, b, right).start()
        ring(pts, 0, mp, b, left).start()
        return 0

    lax.fori_loop(0, blocks, points_in, 0)
    lax.fori_loop(0, vblocks, voxels_out, 0)
    gotv[rows_of(seq, cap), :] = sendv[rows_of(seq, cap), :]
    goti[seq] = sendi[seq]

    def points_on(b, _):
        relay(pts, 0, b)
        return 0

    lax.fori_loop(0, blocks, points_on, 0)
    wait_all(1, gotv, (n - 1) * cap)
    wait_all(2, goti, n - 1)

    def voxels_in(b, _):
        pos = iota((BLK, cap), 0) + b * BLK
        tiles = []
        for t in range(n):
            code = goti[t].astype(F32)
            at = jnp.where(code[2:3, :] > 0.5, code[0:1, :] * 64.0 + code[1:2, :], -1.0).astype(jnp.int32)
            tiles.append(as_mask(pos == at))
        dout[mp, rows_of(b, BLK), :] = dotf(jnp.concatenate(tiles, axis=1), gotv[...]).astype(BF)
        ring(dout, 1, mp, b, right).start()
        ring(dout, 1, mp, b, left).start()
        return 0

    lax.fori_loop(0, blocks, voxels_in, 0)

    wcat = jnp.concatenate([wq[...], wk[...], wv[...]], axis=1)
    ones_lane = as_mask(iota((PATCH, LANES), 1) < 3)
    halves = ((qm0, s0, ds0), (qm1, s1, ds1))

    def normalise(p):
        for b in range(PBLK):
            r = rows_of(p * PBLK + b, BLK)
            c = pl.ds(b * BLK, BLK)
            xb = lanes_of(pts, r).astype(F32)
            xb = xb - jnp.mean(xb, axis=1, keepdims=True)
            inv = lax.rsqrt(jnp.mean(xb * xb, axis=1, keepdims=True) + EPSILON)
            normed = xb * inv
            hidden = normed.astype(BF)
            hid[r, :] = hidden
            invb[r, :] = jnp.broadcast_to(inv, (BLK, LANES))
            own = normed[:, 0:LANES]
            for j in range(1, m):
                own = jnp.where(mp == j, normed[:, j * LANES : (j + 1) * LANES], own)
            d_points[r, :] = own
            proj = dotf(hidden, wcat)
            q, k, val = (proj[:, t * LANES : (t + 1) * LANES].astype(BF) for t in range(3))
            kn[r, :] = k
            vn[r, :] = val
            qf = q.astype(F32).T
            qt[p, :, c] = qf.astype(BF)
            qs = qf * (0.25 * LOG2E)
            high = qs.astype(BF)
            qhl[p, 0:LANES, c] = high
            qhl[p, LANES : 2 * LANES, c] = (qs - high.astype(F32)).astype(BF)
            kt[p, :, c] = k.astype(F32).T.astype(BF)
            vt[p, :, c] = val.astype(F32).T.astype(BF)

    def head_rows(h, base=0):
        return pl.ds(pl.multiple_of(base * LANES + h * HD, HD), HD)

    def scores(p, h, half):
        qm, s = halves[half][:2]
        c = pl.ds(half * QH, QH)
        rmask = (iota((LANES, QH), 0) // HD) == h
        zero = jnp.zeros((LANES, QH), BF)
        qm[0:LANES, :] = jnp.where(rmask, qhl[p, 0:LANES, c], zero)
        qm[LANES : 2 * LANES, :] = jnp.where(rmask, qhl[p, LANES : 2 * LANES, c], zero)
        k = kn[rows_of(p, PATCH), :]
        val = dotf(jnp.concatenate([k, k], axis=1), qm[...])
        s[...] = val
        top[half] = jnp.max(val, axis=0, keepdims=True)

    def forward(p, h, half):
        s = halves[half][1]
        c = pl.ds(half * QH, QH)
        e = jnp.exp2(s[...] - top[half]).astype(BF)
        e_all[p * HEADS + h, :, c] = e
        vt1 = jnp.concatenate([vt[p, head_rows(h), :], jnp.ones((HD, PATCH), BF)], axis=0)
        av = dotf(vt1, e)
        inv = 1.0 / av[HD : HD + 1, :]
        linv[p * HEADS + h, :, c] = inv
        dpt[p, head_rows(h, 3), c] = (av[0:HD, :] * inv).astype(BF)

    def forward_patch(p, _):
        def ready(b, _):
            arrived(pts, 0, p * PBLK + b)
            return 0

        lax.fori_loop(0, PBLK, ready, 0)
        normalise(p)
        scores(p, 0, 0)

        def step(h, _):
            @pl.when(lax.rem(h, 2) == 0)
            def _():
                relay(dout, 1, p * PBLK + h // 2)

            scores(p, h, 1)
            forward(p, h, 0)
            scores(p, jnp.minimum(h + 1, HEADS - 1), 0)
            forward(p, h, 1)
            return 0

        lax.fori_loop(0, HEADS, step, 0)
        return 0

    lax.fori_loop(0, npatch, forward_patch, 0)

    def hop(p, sem, src, dst, to):
        return remote(src, dst, p_send.at[p, sem], p_recv.at[p, sem], "mp", to)

    def hops(p, *which):
        low, high = rows_of(2 * p, PATCH // 2), rows_of(2 * p + 1, PATCH // 2)
        ends = (
            (part.at[opposite, low], rel_l.at[p], right),
            (part.at[opposite, high], rel_r.at[p], left),
            (part.at[right, high], got_l.at[high], right),
            (part.at[left, low], got_r.at[low], left),
            (rel_l.at[p], got_l.at[low], right),
            (rel_r.at[p], got_r.at[high], left),
        )
        return [hop(p, w, *ends[w]) for w in which]

    def hand_on(p):
        low, high = rows_of(2 * p, PATCH // 2), rows_of(2 * p + 1, PATCH // 2)
        in_l, in_r, out_l, out_r = hops(p, 0, 1, 4, 5)
        in_l.wait()
        rel_l[p] = (rel_l[p].astype(F32) + part[right, low, :].astype(F32)).astype(BF)
        out_l.start()
        in_r.wait()
        rel_r[p] = (rel_r[p].astype(F32) + part[left, high, :].astype(F32)).astype(BF)
        out_r.start()

    def backward(p, h, half):
        ds_ref = halves[half][2]
        i = p * HEADS + h
        c = pl.ds(half * QH, QH)
        scaled = (dat[head_rows(h), c].astype(F32) * linv[i, :, c]).astype(BF)
        da = scaled.astype(F32)
        delta = jnp.sum(da * dpt[p, head_rows(h, 3), c].astype(F32), axis=0, keepdims=True)
        d1 = delta.astype(BF).astype(F32)
        d2 = (delta - d1).astype(BF).astype(F32)
        d3 = delta - d1 - d2
        sub = iota((LANES, QH), 0)
        tile = jnp.where(sub // HD == h, jnp.concatenate([da] * HEADS, axis=0), 0.0)
        tail = jnp.where(sub == 0, -d1, jnp.where(sub == 1, -d2, jnp.where(sub == 2, -d3, 0.0)))
        vv = jnp.concatenate([vn[rows_of(p, PATCH), :], ones_lane], axis=1)
        dp = dotf(vv, jnp.concatenate([tile, tail], axis=0).astype(BF))
        ds = e_all[i, :, c] * dp.astype(BF)
        ds_ref[...] = ds
        dpt[p, head_rows(h), c] = (dotf(kt[p, head_rows(h), :], ds) * 0.25).astype(BF)
        return dot_nt(qt[p, head_rows(h), c], ds_ref[...]), dot_nt(scaled, e_all[i, :, c])

    def dout_in(b, _):
        arrived(dout, 1, b)
        return 0

    lax.fori_loop(0, blocks, dout_in, 0)
    ring_sent(pts, 0)
    ring_sent(dout, 1)

    def backward_patch(p, _):
        for b in range(PBLK):
            da = dotf(lanes_of(dout, rows_of(p * PBLK + b, BLK)), wo[...]).astype(BF)
            dat[:, b * BLK : (b + 1) * BLK] = da.astype(F32).T.astype(BF)

        def step(h, _):
            @pl.when(jnp.logical_and(p == 1, h == HEADS // 2))
            def _():
                hand_on(0)

            dk0, dv0 = backward(p, h, 0)
            dk1, dv1 = backward(p, h, 1)
            dpt[p, head_rows(h, 1), :] = ((dk0 + dk1) * 0.25).astype(BF)
            dpt[p, head_rows(h, 2), :] = (dv0 + dv1).astype(BF)
            return 0

        lax.fori_loop(0, HEADS, step, 0)
        for b in range(PBLK):
            r = rows_of(p * PBLK + b, BLK)
            dproj = dpt[p, 0 : 3 * LANES, pl.ds(b * BLK, BLK)].astype(F32).T.astype(BF)
            pd = dot_nt(dproj, wcat).astype(BF)
            xb = lanes_of(pts, r).astype(F32)
            normed = (xb - jnp.mean(xb, axis=1, keepdims=True)) * invb[r, 0:1]
            for j in range(m):
                part[j, r, :] = pd[:, j * LANES : (j + 1) * LANES]
            z = pd.astype(F32) * normed
            zh = z.astype(BF)
            zl = (z - zh.astype(F32)).astype(BF)
            on = jnp.ones((8, pd.shape[1]), BF)
            total = dot_nt(on, pd)
            cross = dot_nt(on, zh) + dot_nt(on, zl)
            stats[p, :, b * BLK : (b + 1) * BLK] = jnp.where(iota((8, BLK), 0) == 0, total, cross)
        for c in hops(p, 0, 1, 2, 3):
            c.start()
        return 0

    lax.fori_loop(0, npatch, backward_patch, 0)

    def stat_copy(i, to):
        return remote(stats, got_s.at[i], s_send.at[i], s_recv.at[i], "mp", to)

    for i, to in enumerate((right, left, opposite)):
        stat_copy(i, to).start()
    upper, lower = 0.0, 0.0
    for p in range(npatch):
        r = pl.ds(p * PATCH, PATCH)
        upper = upper + dotf(dpt[p, 0 : 3 * LANES, :], hid[r, :])
        lower = lower + dotf(dpt[p, 3 * LANES : 4 * LANES, :], lanes_of(dout, r))
    grads[:, 0 : 3 * LANES] = upper.T.astype(BF)
    grads[:, 3 * LANES : 4 * LANES] = lower.T.astype(BF)
    band = grads.shape[0] // n

    def grad_copy(src, dst, peer):
        return remote(src, dst, g_send, g_recv, "seq", peer)

    def grads_out(k, _):
        peer = lax.rem(seq + k, n)
        grad_copy(grads.at[rows_of(peer, band)], got_g.at[seq], peer).start()
        return 0

    lax.fori_loop(1, n, grads_out, 0)
    got_g[seq] = grads[rows_of(seq, band), :]
    hand_on(1)
    others = got_g.at[pl.ds(0, n - 1)]
    grad_copy(others, others, seq).wait()
    total = jnp.zeros((band, grads.shape[1]), F32)
    for k in range(n):
        total = total + got_g[k].astype(F32)
    for t in range(3):
        grad_qkv[:, t, :] = total[:, t * LANES : (t + 1) * LANES]
    grad_out[...] = total[:, 3 * LANES : 4 * LANES]
    for i, to in enumerate((right, left, opposite)):
        stat_copy(i, to).wait()
    scale = 1.0 / (m * LANES)
    for p in range(npatch):
        for c in hops(p, 2, 3, 4, 5):
            c.wait()
        st = (stats[p] + got_s[0, p] + got_s[1, p] + got_s[2, p]) * scale
        for b in range(PBLK):
            r = pl.ds(p * PATCH + b * BLK, BLK)
            mean_grad = lane_copy(st[0:1, b * BLK : (b + 1) * BLK])
            mean_cross = lane_copy(st[1:2, b * BLK : (b + 1) * BLK])
            d_hidden = part[mp, r, :].astype(F32) + got_l[r, :].astype(F32) + got_r[r, :].astype(F32)
            d_points[r, :] = dout[mp, r, :].astype(F32) + invb[r, :] * (
                d_hidden - mean_grad - d_points[r, :] * mean_cross
            )


def local(
    scan_points, send_order, arrive_order, qkv_weight, out_weight, voxel_grads, voxel_shard, voxel_point
):
    n, m = lax.axis_size("seq"), lax.axis_size("mp")
    rows = scan_points.shape[0]
    feats = m * LANES
    grp, cap = rows // n, 2 * voxel_grads.shape[0] // n
    blocks, npatch, band = rows // BLK, rows // PATCH, feats // n
    orders = jnp.stack([send_order, arrive_order, voxel_shard[:, 0], voxel_point]).reshape(4, blocks, BLK)
    vmem, hbm = pl.BlockSpec(memory_space=pltpu.VMEM), pl.BlockSpec(memory_space=pl.ANY)
    dma = pltpu.SemaphoreType.DMA
    col = pltpu.VMEM((rows, LANES), BF)
    per_patch = pltpu.VMEM((npatch, LANES, PATCH), BF)
    half_f = pltpu.VMEM((PATCH, QH), F32)
    half_b = pltpu.VMEM((PATCH, QH), BF)
    masked = pltpu.VMEM((2 * LANES, QH), BF)
    coded = pltpu.VMEM((n, 16, cap), BF)
    full = pltpu.VMEM((m, rows, LANES), BF)
    hop_buf = pltpu.VMEM((npatch, PATCH // 2, LANES), BF)
    return tuple(
        pl.pallas_call(
            layer_kernel,
            out_shape=[
                jax.ShapeDtypeStruct((rows, LANES), F32),
                jax.ShapeDtypeStruct((band, 3, LANES), F32),
                jax.ShapeDtypeStruct((band, LANES), F32),
            ],
            in_specs=[hbm, hbm] + [vmem] * 5,
            out_specs=[vmem] * 3,
            scratch_shapes=[
                col, col, col, pltpu.VMEM((n * cap, LANES), BF), coded,
                col, pltpu.VMEM((n * cap, LANES), BF), coded, pltpu.VMEM((blocks, BLK), jnp.int32),
                full, full, pltpu.VMEM((rows, feats), BF), col, col,
                pltpu.VMEM((npatch, 2 * LANES, PATCH), BF),
                per_patch, per_patch, per_patch, pltpu.VMEM((LANES, PATCH), BF),
                pltpu.VMEM((npatch, 4 * LANES, PATCH), BF),
                masked, masked, half_f, half_f,
                pltpu.VMEM((npatch * HEADS, PATCH, PATCH), BF),
                half_b, half_b,
                pltpu.VMEM((2, 1, QH), F32),
                pltpu.VMEM((npatch * HEADS, 1, PATCH), F32),
                pltpu.VMEM((feats, 4 * LANES), BF),
                pltpu.VMEM((npatch, 8, PATCH), F32),
                pltpu.VMEM((rows, LANES), F32),
                hop_buf, hop_buf,
                pltpu.VMEM((m - 1, npatch, 8, PATCH), F32),
                pltpu.VMEM((n, band, 4 * LANES), BF),
                dma((2,)), dma((3,)), dma((3,)), dma((2,)), dma((2, m, blocks)),
                dma((npatch, 6)), dma((npatch, 6)), dma((m - 1,)), dma((m - 1,)), dma(()), dma(()),
            ],
            compiler_params=pltpu.CompilerParams(
                collective_id=0, has_side_effects=True, vmem_limit_bytes=67043328
            ),
            name="layer",
        )(
            scan_points, voxel_grads, orders,
            qkv_weight[:, 0], qkv_weight[:, 1], qkv_weight[:, 2], out_weight,
        )
    )


def solution(mesh):
    in_specs = (
        P("seq", None), P("seq"), P("seq"), P(None, None, "mp"), P(None, "mp"),
        P("seq", None), P("seq", None), P("seq"),
    )
    out_specs = (P("seq", "mp"), P("seq", None, "mp"), P("seq", "mp"))
    return jax.shard_map(local, mesh=mesh, in_specs=in_specs, out_specs=out_specs, check_vma=False)
```

time: 468 us -> 141 us (0.30); the launches traced: 460 us -> 140 us
  matrix products: 132 us -> 0 us
  Pallas kernels: 0 us -> 130 us
  waiting for transfers between devices: 114 us -> 0 us
  other arithmetic: 96.4 us -> 0.62 us
  local copies, waits for them, and re-layouts: 64.7 us -> 8.81 us
  starting transfers between devices: 24.2 us -> 0 us
  between operations: 16 us -> 0.65 us
  loops' own time: 12 us -> 0 us
    pallas_call x0 -> x1, Pallas kernels: none -> 130 us  [local(): pl.pallas_call(layer_kernel, out_shape=[jax.ShapeDtypeStruct((rows, LANES...]
    dot_general x15 -> x0, matrix products: 103 us -> none  [the longest x2 26 us: patch_pass(): jnp.einsum('qhc,khc->hqk', grad_heads, value_heads, preferred_element_typ...]
    reduce_scatter x1 -> x0, waiting for transfers between devices: 67.1 us -> none  [local(): lax.psum_scatter(jnp.concatenate([upper, lower[:, None, :]], axis=1).asty...]
    all_to_all x3 -> x0, waiting for transfers between devices: 47 us -> none  [the longest x1 31.7 us: local(): lax.all_to_all(send_rows, 'seq', split_axis=0, concat_axis=0, tiled=True)]
    convert_element_type x5 -> x0, other arithmetic: 37.8 us -> none  [the longest x2 35.6 us: patch_pass(): prob_rounded = probabilities.astype(jnp.bfloat16)]
    scatter-add x1 -> x0, other arithmetic: 30.5 us -> none  [local(): jax.ops.segment_sum(got_rows.astype(jnp.float32), got_index, num_segments...]
    sub x2 -> x0, matrix products: 29.1 us -> none  [patch_pass(): weights_exp = jnp.exp(scores - row_max)]
    all_to_all x3 -> x0, starting transfers between devices: 23.8 us -> none  [the longest x1 9.43 us: local(): lax.all_to_all(send_index, 'seq', split_axis=0, concat_axis=0, tiled=True)]
  transfers between devices with their start and end apart: 5 -> 0, of which waited for: 3 -> 0; matrix products, arithmetic and copies ran while one was open for 12% -> 0% of each run, Pallas kernels for 0% -> 0%
where the time goes in v2:
time: 141 us; the launch traced here: 140 us
  Pallas kernels  130 us (92%)
  local copies, waits for them, and re-layouts  8.81 us (6%)
    pallas_call x1, Pallas kernels, local(): pl.pallas_call(layer_kernel, out_shape=[jax.ShapeDtypeStruct((rows, LANES...  130 us
    unnamed x5, local copies, waits for them, and re-layouts  3.56 us

profile of v2, /device:TPU:1, one launch (start us, length us, event | category | flops | bytes accessed | tf_op | source)
XLA Modules:
  0.0 140.0 jit_solution(16094774094272206021)
XLA Ops:
  0.6 0.7 stack.14
  1.3 0.7 stack.15
  2.0 0.7 copy.14
  2.7 0.7 stack.17
  3.4 0.6 pad_add_fusion.orders
  4.0 1.8 %slice_bitcast_fusion = (bf16[512,128]{1,0:T(8,128)(2,1)}, bf16[512,128]{1,0:T(8,128)(2,1)}, bf16[512,128]{1,0:T(8,128)(2,1)}) fusion(bf16[512,3,128]{2,0,1:T(8,128)(2,1)} %param.11), kind=kLoop, calls=%fused_computation | loop fusion | bytes 786432 | tf_op jit(solution)/shard_map/squeeze | solution.py:509
  5.8 129.9 %layer.1 = (f32[2048,128]{1,0:T(8,128)}, f32[16,3,128]{2,1,0:T(4,128)}, f32[16,128]{1,0:T(8,128)}) custom-call(bf16[2048,512]{1,0:T(8,128)(2,1)} %scan.1, bf16[2048,512]{1,0:T(8,128)(2,1)} %voxels.1, s32[4,8,256]{2,1,0:T(8,128)} %pad_add_fusion.orders, bf16[512,128]{1,0:T(8,128)(2,1)} %get-tuple-element.7.wq, bf16[512,128]{1,0:T(8,128)(2,1)} %get-tuple-element.8.wk, ...), custom_call_target="tpu_custom_call" | custom-call | tf_op jit(solution)/shard_map/layer/pallas_call | solution.py:473
  135.7 0.0 copy-start
  135.7 1.4 copy.11
  137.1 2.3 %copy.17 = f32[2048,128]{1,0:T(8,128)} copy(f32[2048,128]{1,0:T(8,128)} %get-tuple-element.12) | data formatting | bytes 2097152
  139.4 0.0 copy-done
  139.4 0.6 copy.18
Async XLA Ops:
  135.7 3.6 %copy-start = (f32[16,128]{1,0:T(8,128)S(1)}, f32[16,128]{1,0:T(8,128)}, u32[]{:S(2)}) copy-start(f32[16,128]{1,0:T(8,128)} %get-tuple-element.14) | copy-start | bytes 24580

commit v3 on v2

--- a/solution.py
+++ b/solution.py
@@ -35,14 +35,33 @@
     return jnp.where(cond, 1.0, 0.0).astype(BF)
 
 
+def small_iota(shape, axis):
+    return iota(shape, axis).astype(F32).astype(BF)
+
+
 def lane_copy(row):
     return jnp.broadcast_to(row.astype(F32), (LANES, BLK)).T
 
 
+def block_row(ref, b):
+    per = BLK // LANES
+    return jnp.concatenate([ref[pl.ds(b * per + u, 1), :] for u in range(per)], axis=1)
+
+
 def select_rows(order_row, count):
-    want = lane_copy(order_row).astype(jnp.int32)
-    lane = iota((BLK, LANES), 1)
-    return jnp.concatenate([as_mask(want == lane + c * LANES) for c in range(count // LANES)], axis=1)
+    want = lane_copy(order_row)
+    high = jnp.floor(want * (1.0 / LANES))
+    low = (want - high * LANES).astype(BF)
+    high = high.astype(BF)
+    zero = jnp.zeros((BLK, LANES), BF)
+    here = jnp.where(low == small_iota((BLK, LANES), 1), jnp.ones((BLK, LANES), BF), zero)
+    return jnp.concatenate([jnp.where(high == c, here, zero) for c in range(count // LANES)], axis=1)
+
+
+def hits(position, b):
+    shape = (BLK, position.shape[1])
+    near = jnp.clip(position.astype(F32) - (b * BLK).astype(F32), -1.0, float(BLK)).astype(BF)
+    return jnp.where(small_iota(shape, 0) == near, jnp.ones(shape, BF), jnp.zeros(shape, BF))
 
 
 def lanes_of(ref, r):
@@ -61,9 +80,9 @@
 
 
 def layer_kernel(
-    scan, voxels, orders, wq, wk, wv, wo,
+    scan, voxels, send_order, arrive_order, point, shard, w, wo,
     d_points, grad_qkv, grad_out,
-    x, v, sendp, sendv, sendi, gotp, gotv, goti, place,
+    x, v, sendp, sendv, sendi, gotp, gotv, goti, place, at_all,
     pts, dout, hid, kn, vn, qhl, qt, kt, vt, dat, dpt, qm0, qm1, s0, s1, e_all, ds0, ds1, top, linv,
     grads, stats, invb, rel_l, rel_r, got_s, got_g,
     in_sem, send_sem, recv_sem, ring_send, ring_recv, p_send, p_recv, s_send, s_recv, g_send, g_recv,
@@ -77,7 +96,6 @@
     blocks = rows // BLK
     right, left, opposite = lax.rem(mp + 1, m), lax.rem(mp + m - 1, m), lax.rem(mp + 2, m)
     part, got_l, got_r = pts, x, v
-    send_order, arrive_order, shard, point = (orders.at[i] for i in range(4))
 
     mine = pl.ds(pl.multiple_of(mp * LANES, LANES), LANES)
     in_x = pltpu.make_async_copy(scan.at[:, mine], x, in_sem.at[0])
@@ -93,37 +111,17 @@
     def send(src, dst, kind, peer):
         return remote(src, dst, send_sem.at[kind], recv_sem.at[kind], "seq", peer)
 
-    in_x.wait()
-    pl.semaphore_wait(barrier, n + m - 2)
-    per = BLK // grp
-
-    def points_out(i, _):
-        b = lax.rem(i + seq // per, blocks)
-        hot = select_rows(send_order[pl.ds(b, 1), :], rows)
-        sendp[rows_of(b, BLK), :] = dotf(hot, x[...]).astype(BF)
-        for u in range(per):
-            peer = b * per + u
-
-            @pl.when(peer != seq)
-            def _():
-                send(sendp.at[rows_of(peer, grp)], gotp.at[rows_of(seq, grp)], 0, peer).start()
-
-        return 0
-
-    lax.fori_loop(0, blocks, points_out, 0)
-    gotp[rows_of(seq, grp), :] = sendp[rows_of(seq, grp), :]
-
     tri = as_mask(iota((BLK, BLK), 0) < iota((BLK, BLK), 1))
     carry = jnp.zeros((n, 1), F32)
     codes = jnp.zeros((3 * n, cap), F32)
     for b in range(blocks):
-        target = shard[b : b + 1, :]
+        target = shard[:, b * BLK : (b + 1) * BLK]
         hot = jnp.where(iota((n, BLK), 0) == target, 1.0, 0.0)
         before = dotf(hot.astype(BF), tri) + carry
         rank = jnp.sum(before * hot, axis=0, keepdims=True)
         carry = carry + jnp.sum(hot, axis=1, keepdims=True)
         place[b : b + 1, :] = target * cap + rank.astype(jnp.int32)
-        where_to = point[b : b + 1, :]
+        where_to = block_row(point, b)
         high = (where_to // 64).astype(F32)
         low = (where_to % 64).astype(F32)
         slot = as_mask(iota((cap, BLK), 0) == rank.astype(jnp.int32))
@@ -133,14 +131,33 @@
     for t in range(n):
         a, b, c = codes[t : t + 1], codes[n + t : n + t + 1], codes[2 * n + t : 2 * n + t + 1]
         sendi[t] = jnp.where(sub16 == 0, a, jnp.where(sub16 == 1, b, c)).astype(BF)
+    in_x.wait()
+    pl.semaphore_wait(barrier, n + m - 2)
+    per = BLK // grp
+
+    def points_out(i, _):
+        b = lax.rem(i + seq // per, blocks)
+        hot = select_rows(block_row(send_order, b), rows)
+        sendp[rows_of(b, BLK), :] = dotf(hot, x[...]).astype(BF)
+        for u in range(per):
+            peer = b * per + u
+
+            @pl.when(peer != seq)
+            def _():
+                send(sendp.at[rows_of(peer, grp)], gotp.at[rows_of(seq, grp)], 0, peer).start()
+
+        return 0
+
+    lax.fori_loop(0, blocks, points_out, 0)
+    gotp[rows_of(seq, grp), :] = sendp[rows_of(seq, grp), :]
+
     in_v.wait()
     per_v = BLK // cap
     vblocks = n // per_v
 
     def voxels_out(i, _):
         b = lax.rem(i + seq // per_v, vblocks)
-        slot = iota((BLK, BLK), 0) + b * BLK
-        hot = jnp.concatenate([as_mask(slot == place[c : c + 1, :]) for c in range(blocks)], axis=1)
+        hot = jnp.concatenate([hits(place[c : c + 1, :], b) for c in range(blocks)], axis=1)
         sendv[rows_of(b, BLK), :] = dotf(hot, v[...]).astype(BF)
         for u in range(per_v):
             peer = b * per_v + u
@@ -151,6 +168,10 @@
                 send(sendi.at[peer], goti.at[seq], 2, peer).start()
 
         return 0
+
+    lax.fori_loop(0, vblocks, voxels_out, 0)
+    gotv[rows_of(seq, cap), :] = sendv[rows_of(seq, cap), :]
+    goti[seq] = sendi[seq]
 
     def wait_all(kind, ref, size):
         other = ref.at[pl.ds(0, size)]
@@ -193,40 +214,30 @@
     wait_all(0, gotp, (n - 1) * grp)
 
     def points_in(b, _):
-        hot = select_rows(arrive_order[pl.ds(b, 1), :], rows)
+        hot = select_rows(block_row(arrive_order, b), rows)
         pts[mp, rows_of(b, BLK), :] = dotf(hot, gotp[...]).astype(BF)
         ring(pts, 0, mp, b, right).start()
         ring(pts, 0, mp, b, left).start()
         return 0
 
     lax.fori_loop(0, blocks, points_in, 0)
-    lax.fori_loop(0, vblocks, voxels_out, 0)
-    gotv[rows_of(seq, cap), :] = sendv[rows_of(seq, cap), :]
-    goti[seq] = sendi[seq]
-
-    def points_on(b, _):
-        relay(pts, 0, b)
-        return 0
-
-    lax.fori_loop(0, blocks, points_on, 0)
     wait_all(1, gotv, (n - 1) * cap)
     wait_all(2, goti, n - 1)
+    for t in range(n):
+        code = goti[t].astype(F32)
+        at_all[t : t + 1, :] = jnp.where(code[2:3, :] > 0.5, code[0:1, :] * 64.0 + code[1:2, :], -1.0)
 
     def voxels_in(b, _):
-        pos = iota((BLK, cap), 0) + b * BLK
-        tiles = []
-        for t in range(n):
-            code = goti[t].astype(F32)
-            at = jnp.where(code[2:3, :] > 0.5, code[0:1, :] * 64.0 + code[1:2, :], -1.0).astype(jnp.int32)
-            tiles.append(as_mask(pos == at))
-        dout[mp, rows_of(b, BLK), :] = dotf(jnp.concatenate(tiles, axis=1), gotv[...]).astype(BF)
+        hot = jnp.concatenate([hits(at_all[t : t + 1, :], b) for t in range(n)], axis=1)
+        dout[mp, rows_of(b, BLK), :] = dotf(hot, gotv[...]).astype(BF)
         ring(dout, 1, mp, b, right).start()
         ring(dout, 1, mp, b, left).start()
+        relay(pts, 0, b)
         return 0
 
     lax.fori_loop(0, blocks, voxels_in, 0)
 
-    wcat = jnp.concatenate([wq[...], wk[...], wv[...]], axis=1)
+    wcat = jnp.concatenate([w[t] for t in range(3)], axis=1)
     ones_lane = as_mask(iota((PATCH, LANES), 1) < 3)
     halves = ((qm0, s0, ds0), (qm1, s1, ds1))
 
@@ -425,18 +436,11 @@
     lax.fori_loop(1, n, grads_out, 0)
     got_g[seq] = grads[rows_of(seq, band), :]
     hand_on(1)
-    others = got_g.at[pl.ds(0, n - 1)]
-    grad_copy(others, others, seq).wait()
-    total = jnp.zeros((band, grads.shape[1]), F32)
-    for k in range(n):
-        total = total + got_g[k].astype(F32)
-    for t in range(3):
-        grad_qkv[:, t, :] = total[:, t * LANES : (t + 1) * LANES]
-    grad_out[...] = total[:, 3 * LANES : 4 * LANES]
     for i, to in enumerate((right, left, opposite)):
         stat_copy(i, to).wait()
     scale = 1.0 / (m * LANES)
-    for p in range(npatch):
+
+    def finish(p):
         for c in hops(p, 2, 3, 4, 5):
             c.wait()
         st = (stats[p] + got_s[0, p] + got_s[1, p] + got_s[2, p]) * scale
@@ -449,6 +453,17 @@
                 d_hidden - mean_grad - d_points[r, :] * mean_cross
             )
 
+    finish(0)
+    others = got_g.at[pl.ds(0, n - 1)]
+    grad_copy(others, others, seq).wait()
+    total = jnp.zeros((band, grads.shape[1]), F32)
+    for k in range(n):
+        total = total + got_g[k].astype(F32)
+    for t in range(3):
+        grad_qkv[t] = total[:, t * LANES : (t + 1) * LANES]
+    grad_out[...] = total[:, 3 * LANES : 4 * LANES]
+    finish(1)
+
 
 def local(
     scan_points, send_order, arrive_order, qkv_weight, out_weight, voxel_grads, voxel_shard, voxel_point
@@ -458,7 +473,6 @@
     feats = m * LANES
     grp, cap = rows // n, 2 * voxel_grads.shape[0] // n
     blocks, npatch, band = rows // BLK, rows // PATCH, feats // n
-    orders = jnp.stack([send_order, arrive_order, voxel_shard[:, 0], voxel_point]).reshape(4, blocks, BLK)
     vmem, hbm = pl.BlockSpec(memory_space=pltpu.VMEM), pl.BlockSpec(memory_space=pl.ANY)
     dma = pltpu.SemaphoreType.DMA
     col = pltpu.VMEM((rows, LANES), BF)
@@ -469,19 +483,19 @@
     coded = pltpu.VMEM((n, 16, cap), BF)
     full = pltpu.VMEM((m, rows, LANES), BF)
     hop_buf = pltpu.VMEM((npatch, PATCH // 2, LANES), BF)
-    return tuple(
+    d_points, grad_qkv, grad_out = (
         pl.pallas_call(
             layer_kernel,
             out_shape=[
                 jax.ShapeDtypeStruct((rows, LANES), F32),
-                jax.ShapeDtypeStruct((band, 3, LANES), F32),
+                jax.ShapeDtypeStruct((3, band, LANES), F32),
                 jax.ShapeDtypeStruct((band, LANES), F32),
             ],
-            in_specs=[hbm, hbm] + [vmem] * 5,
+            in_specs=[hbm, hbm] + [vmem] * 6,
             out_specs=[vmem] * 3,
             scratch_shapes=[
                 col, col, col, pltpu.VMEM((n * cap, LANES), BF), coded,
-                col, pltpu.VMEM((n * cap, LANES), BF), coded, pltpu.VMEM((blocks, BLK), jnp.int32),
+                col, pltpu.VMEM((n * cap, LANES), BF), coded, pltpu.VMEM((blocks, BLK), jnp.int32), pltpu.VMEM((n, cap), F32),
                 full, full, pltpu.VMEM((rows, feats), BF), col, col,
                 pltpu.VMEM((npatch, 2 * LANES, PATCH), BF),
                 per_patch, per_patch, per_patch, pltpu.VMEM((LANES, PATCH), BF),
@@ -505,10 +519,12 @@
             ),
             name="layer",
         )(
-            scan_points, voxel_grads, orders,
-            qkv_weight[:, 0], qkv_weight[:, 1], qkv_weight[:, 2], out_weight,
+            scan_points, voxel_grads,
+            send_order.reshape(-1, LANES), arrive_order.reshape(-1, LANES), voxel_point.reshape(-1, LANES),
+            voxel_shard.reshape(1, -1), jnp.transpose(qkv_weight, (1, 0, 2)), out_weight,
         )
     )
+    return d_points, jnp.transpose(grad_qkv, (1, 0, 2)), grad_out
 
 
 def solution(mesh):

time: 141 us -> 133 us (0.943)
  local copies, waits for them, and re-layouts: 8.81 us -> 3.49 us
    another operation x3 -> x0, local copies, waits for them, and re-layouts: 2.1 us -> none  [local(): jnp.stack([send_order, arrive_order, voxel_shard[:, 0], voxel_point])]
    squeeze x1 -> x0, local copies, waits for them, and re-layouts: 1.78 us -> none  [local(): qkv_weight[:, 2]]
    unnamed x5 -> x7, local copies, waits for them, and re-layouts: 3.56 us -> 3.49 us
where the time goes in v3:
time: 133 us
  Pallas kernels  129 us (97%)
  local copies, waits for them, and re-layouts  3.49 us (3%)
    pallas_call x1, Pallas kernels, local(): pl.pallas_call(layer_kernel, out_shape=[jax.ShapeDtypeStruct((rows, LANES...  129 us
    unnamed x7, local copies, waits for them, and re-layouts  3.49 us

profile of v3, /device:TPU:1, one launch (start us, length us, event | category | flops | bytes accessed | tf_op | source)
XLA Modules:
  0.0 132.6 jit_solution(1305531901871560284)
XLA Ops:
  0.6 128.5 %layer.1 = (f32[2048,128]{1,0:T(8,128)}, f32[3,16,128]{2,1,0:T(8,128)}, f32[16,128]{1,0:T(8,128)}) custom-call(bf16[2048,512]{1,0:T(8,128)(2,1)} %scan.1, bf16[2048,512]{1,0:T(8,128)(2,1)} %voxels.1, s32[16,128]{1,0:T(8,128)} %bitcast.8, s32[16,128]{1,0:T(8,128)} %bitcast.9, s32[16,128]{1,0:T(8,128)} %bitcast.10, s32[1,2048]{1,0:T(1,128)} %bitcast.11, ...), custom_call_target="tpu_custom_call" | custom-call | tf_op jit(solution)/shard_map/layer/pallas_call | solution.py:487
  129.1 0.0 copy-start
  129.2 0.0 copy-start.1
  129.2 2.3 %copy.14 = f32[2048,128]{1,0:T(8,128)} copy(f32[2048,128]{1,0:T(8,128)} %get-tuple-element.12) | data formatting | bytes 2097152
  131.4 0.0 copy-done
  131.4 0.6 copy.15
  132.0 0.0 copy-done.1
  132.1 0.6 copy.16
Async XLA Ops:
  129.1 2.3 %copy-start = (f32[3,16,128]{2,1,0:T(8,128)S(1)}, f32[3,16,128]{2,1,0:T(8,128)}, u32[]{:S(2)}) copy-start(f32[3,16,128]{2,1,0:T(8,128)} %get-tuple-element.7) | copy-start | bytes 73732
  129.2 2.9 %copy-start.1 = (f32[16,128]{1,0:T(8,128)S(1)}, f32[16,128]{1,0:T(8,128)}, u32[]{:S(2)}) copy-start(f32[16,128]{1,0:T(8,128)} %get-tuple-element.14) | copy-start | bytes 24580

commit v4 on v3

--- a/solution.py
+++ b/solution.py
@@ -12,6 +12,7 @@
 HEADS = LANES // HD
 PBLK = PATCH // BLK
 QH = 512
+CH = 256
 EPSILON = 1e-05
 LOG2E = 1.4426950408889634
 BF = jnp.bfloat16
@@ -83,7 +84,7 @@
     scan, voxels, send_order, arrive_order, point, shard, w, wo,
     d_points, grad_qkv, grad_out,
     x, v, sendp, sendv, sendi, gotp, gotv, goti, place, at_all,
-    pts, dout, hid, kn, vn, qhl, qt, kt, vt, dat, dpt, qm0, qm1, s0, s1, e_all, ds0, ds1, top, linv,
+    pts, dout, hid, kn, vn, qhl, qt, kt, vt, dat, dpt, qm0, qm1, s0, s1, e_all, ds0, ds1, top, linv, dst, est,
     grads, stats, invb, rel_l, rel_r, got_s, got_g,
     in_sem, send_sem, recv_sem, ring_send, ring_recv, p_send, p_recv, s_send, s_recv, g_send, g_recv,
 ):
@@ -132,15 +133,20 @@
         a, b, c = codes[t : t + 1], codes[n + t : n + t + 1], codes[2 * n + t : 2 * n + t + 1]
         sendi[t] = jnp.where(sub16 == 0, a, jnp.where(sub16 == 1, b, c)).astype(BF)
     in_x.wait()
-    pl.semaphore_wait(barrier, n + m - 2)
     per = BLK // grp
 
-    def points_out(i, _):
-        b = lax.rem(i + seq // per, blocks)
+    def ordered(i):
+        return lax.rem(i + seq // per, blocks)
+
+    def points_pick(i, _):
+        b = ordered(i)
         hot = select_rows(block_row(send_order, b), rows)
         sendp[rows_of(b, BLK), :] = dotf(hot, x[...]).astype(BF)
+        return 0
+
+    def points_send(i, _):
         for u in range(per):
-            peer = b * per + u
+            peer = ordered(i) * per + u
 
             @pl.when(peer != seq)
             def _():
@@ -148,7 +154,15 @@
 
         return 0
 
-    lax.fori_loop(0, blocks, points_out, 0)
+    def points_out(i, _):
+        points_pick(i, 0)
+        points_send(i, 0)
+        return 0
+
+    lax.fori_loop(0, blocks // 2, points_pick, 0)
+    pl.semaphore_wait(barrier, n + m - 2)
+    lax.fori_loop(0, blocks // 2, points_send, 0)
+    lax.fori_loop(blocks // 2, blocks, points_out, 0)
     gotp[rows_of(seq, grp), :] = sendp[rows_of(seq, grp), :]
 
     in_v.wait()
@@ -228,11 +242,11 @@
         at_all[t : t + 1, :] = jnp.where(code[2:3, :] > 0.5, code[0:1, :] * 64.0 + code[1:2, :], -1.0)
 
     def voxels_in(b, _):
+        relay(pts, 0, b)
         hot = jnp.concatenate([hits(at_all[t : t + 1, :], b) for t in range(n)], axis=1)
         dout[mp, rows_of(b, BLK), :] = dotf(hot, gotv[...]).astype(BF)
         ring(dout, 1, mp, b, right).start()
         ring(dout, 1, mp, b, left).start()
-        relay(pts, 0, b)
         return 0
 
     lax.fori_loop(0, blocks, voxels_in, 0)
@@ -363,7 +377,13 @@
         ds = e_all[i, :, c] * dp.astype(BF)
         ds_ref[...] = ds
         dpt[p, head_rows(h), c] = (dotf(kt[p, head_rows(h), :], ds) * 0.25).astype(BF)
-        return dot_nt(qt[p, head_rows(h), c], ds_ref[...]), dot_nt(scaled, e_all[i, :, c])
+        for u in range(PATCH // CH):
+            r = pl.ds(u * CH, CH)
+            dst[half, :, r] = ds_ref[r, :].T
+        for u in range(PATCH // CH):
+            r = pl.ds(u * CH, CH)
+            est[half, :, r] = e_all[i, r, c].T
+        return dotf(qt[p, head_rows(h), c], dst[half]), dotf(scaled, est[half])
 
     def dout_in(b, _):
         arrived(dout, 1, b)
@@ -372,6 +392,9 @@
     lax.fori_loop(0, blocks, dout_in, 0)
     ring_sent(pts, 0)
     ring_sent(dout, 1)
+
+    def stat_copy(p, i, to):
+        return remote(stats.at[p], got_s.at[p, i], s_send.at[p, i], s_recv.at[p, i], "mp", to)
 
     def backward_patch(p, _):
         for b in range(PBLK):
@@ -394,28 +417,22 @@
             r = rows_of(p * PBLK + b, BLK)
             dproj = dpt[p, 0 : 3 * LANES, pl.ds(b * BLK, BLK)].astype(F32).T.astype(BF)
             pd = dot_nt(dproj, wcat).astype(BF)
-            xb = lanes_of(pts, r).astype(F32)
-            normed = (xb - jnp.mean(xb, axis=1, keepdims=True)) * invb[r, 0:1]
             for j in range(m):
                 part[j, r, :] = pd[:, j * LANES : (j + 1) * LANES]
-            z = pd.astype(F32) * normed
-            zh = z.astype(BF)
-            zl = (z - zh.astype(F32)).astype(BF)
-            on = jnp.ones((8, pd.shape[1]), BF)
-            total = dot_nt(on, pd)
-            cross = dot_nt(on, zh) + dot_nt(on, zl)
-            stats[p, :, b * BLK : (b + 1) * BLK] = jnp.where(iota((8, BLK), 0) == 0, total, cross)
-        for c in hops(p, 0, 1, 2, 3):
-            c.start()
+            if b % 2 == 1:
+                for c in hops(p, *((0, 3), (1, 2))[b // 2]):
+                    c.start()
+            gram = dot_nt(pd, hid[r, :])
+            cross = jnp.sum(jnp.where(iota((BLK, BLK), 0) == iota((BLK, BLK), 1), gram, 0.0), axis=0, keepdims=True)
+            total = dot_nt(jnp.ones((8, pd.shape[1]), BF), pd)
+            stats[p, 2 * b : 2 * b + 1, :] = total[0:1]
+            stats[p, 2 * b + 1 : 2 * b + 2, :] = cross
+        for i, to in enumerate((right, left, opposite)):
+            stat_copy(p, i, to).start()
         return 0
 
     lax.fori_loop(0, npatch, backward_patch, 0)
 
-    def stat_copy(i, to):
-        return remote(stats, got_s.at[i], s_send.at[i], s_recv.at[i], "mp", to)
-
-    for i, to in enumerate((right, left, opposite)):
-        stat_copy(i, to).start()
     upper, lower = 0.0, 0.0
     for p in range(npatch):
         r = pl.ds(p * PATCH, PATCH)
@@ -436,18 +453,18 @@
     lax.fori_loop(1, n, grads_out, 0)
     got_g[seq] = grads[rows_of(seq, band), :]
     hand_on(1)
-    for i, to in enumerate((right, left, opposite)):
-        stat_copy(i, to).wait()
     scale = 1.0 / (m * LANES)
 
     def finish(p):
         for c in hops(p, 2, 3, 4, 5):
             c.wait()
-        st = (stats[p] + got_s[0, p] + got_s[1, p] + got_s[2, p]) * scale
+        for i, to in enumerate((right, left, opposite)):
+            stat_copy(p, i, to).wait()
+        st = (stats[p] + got_s[p, 0] + got_s[p, 1] + got_s[p, 2]) * scale
         for b in range(PBLK):
             r = pl.ds(p * PATCH + b * BLK, BLK)
-            mean_grad = lane_copy(st[0:1, b * BLK : (b + 1) * BLK])
-            mean_cross = lane_copy(st[1:2, b * BLK : (b + 1) * BLK])
+            mean_grad = lane_copy(st[2 * b : 2 * b + 1])
+            mean_cross = lane_copy(st[2 * b + 1 : 2 * b + 2])
             d_hidden = part[mp, r, :].astype(F32) + got_l[r, :].astype(F32) + got_r[r, :].astype(F32)
             d_points[r, :] = dout[mp, r, :].astype(F32) + invb[r, :] * (
                 d_hidden - mean_grad - d_points[r, :] * mean_cross
@@ -504,15 +521,15 @@
                 pltpu.VMEM((npatch * HEADS, PATCH, PATCH), BF),
                 half_b, half_b,
                 pltpu.VMEM((2, 1, QH), F32),
-                pltpu.VMEM((npatch * HEADS, 1, PATCH), F32),
+                pltpu.VMEM((npatch * HEADS, 1, PATCH), F32), pltpu.VMEM((2, QH, PATCH), BF), pltpu.VMEM((2, QH, PATCH), BF),
                 pltpu.VMEM((feats, 4 * LANES), BF),
-                pltpu.VMEM((npatch, 8, PATCH), F32),
+                pltpu.VMEM((npatch, 2 * PBLK, BLK), F32),
                 pltpu.VMEM((rows, LANES), F32),
                 hop_buf, hop_buf,
-                pltpu.VMEM((m - 1, npatch, 8, PATCH), F32),
+                pltpu.VMEM((npatch, m - 1, 2 * PBLK, BLK), F32),
                 pltpu.VMEM((n, band, 4 * LANES), BF),
                 dma((2,)), dma((3,)), dma((3,)), dma((2,)), dma((2, m, blocks)),
-                dma((npatch, 6)), dma((npatch, 6)), dma((m - 1,)), dma((m - 1,)), dma(()), dma(()),
+                dma((npatch, 6)), dma((npatch, 6)), dma((npatch, m - 1)), dma((npatch, m - 1)), dma(()), dma(()),
             ],
             compiler_params=pltpu.CompilerParams(
                 collective_id=0, has_side_effects=True, vmem_limit_bytes=67043328

time: 133 us -> 119 us (0.89)
  Pallas kernels: 129 us -> 115 us
    pallas_call x1, Pallas kernels: 129 us -> 115 us  [local(): pl.pallas_call(layer_kernel, out_shape=[jax.ShapeDtypeStruct((rows, LANES...]
where the time goes in v4:
time: 119 us
  Pallas kernels  115 us (97%)
  local copies, waits for them, and re-layouts  3.49 us (3%)
    pallas_call x1, Pallas kernels, local(): pl.pallas_call(layer_kernel, out_shape=[jax.ShapeDtypeStruct((rows, LANES...  115 us
    unnamed x7, local copies, waits for them, and re-layouts  3.49 us

profile of v4, /device:TPU:1, one launch (start us, length us, event | category | flops | bytes accessed | tf_op | source)
XLA Modules:
  0.0 119.2 jit_solution(13773555672007618982)
XLA Ops:
  0.6 115.0 %layer.1 = (f32[2048,128]{1,0:T(8,128)}, f32[3,16,128]{2,1,0:T(8,128)}, f32[16,128]{1,0:T(8,128)}) custom-call(bf16[2048,512]{1,0:T(8,128)(2,1)} %scan.1, bf16[2048,512]{1,0:T(8,128)(2,1)} %voxels.1, s32[16,128]{1,0:T(8,128)} %bitcast.8, s32[16,128]{1,0:T(8,128)} %bitcast.9, s32[16,128]{1,0:T(8,128)} %bitcast.10, s32[1,2048]{1,0:T(1,128)} %bitcast.11, ...), custom_call_target="tpu_custom_call" | custom-call | tf_op jit(solution)/shard_map/layer/pallas_call | solution.py:504
  115.7 0.0 copy-start
  115.7 0.0 copy-start.1
  115.7 2.3 %copy.14 = f32[2048,128]{1,0:T(8,128)} copy(f32[2048,128]{1,0:T(8,128)} %get-tuple-element.12) | data formatting | bytes 2097152
  118.0 0.0 copy-done
  118.0 0.6 copy.15
  118.6 0.0 copy-done.1
  118.6 0.6 copy.16
Async XLA Ops:
  115.7 2.3 %copy-start = (f32[3,16,128]{2,1,0:T(8,128)S(1)}, f32[3,16,128]{2,1,0:T(8,128)}, u32[]{:S(2)}) copy-start(f32[3,16,128]{2,1,0:T(8,128)} %get-tuple-element.7) | copy-start | bytes 73732
  115.7 2.9 %copy-start.1 = (f32[16,128]{1,0:T(8,128)S(1)}, f32[16,128]{1,0:T(8,128)}, u32[]{:S(2)}) copy-start(f32[16,128]{1,0:T(8,128)} %get-tuple-element.14) | copy-start | bytes 24580

commit v5 on v4

--- a/solution.py
+++ b/solution.py
@@ -82,8 +82,8 @@
 
 def layer_kernel(
     scan, voxels, send_order, arrive_order, point, shard, w, wo,
-    d_points, grad_qkv, grad_out,
-    x, v, sendp, sendv, sendi, gotp, gotv, goti, place, at_all,
+    d_high, d_low, grad_qkv, grad_out,
+    normq, x, v, sendp, sendv, sendi, gotp, gotv, goti, place, at_all,
     pts, dout, hid, kn, vn, qhl, qt, kt, vt, dat, dpt, qm0, qm1, s0, s1, e_all, ds0, ds1, top, linv, dst, est,
     grads, stats, invb, rel_l, rel_r, got_s, got_g,
     in_sem, send_sem, recv_sem, ring_send, ring_recv, p_send, p_recv, s_send, s_recv, g_send, g_recv,
@@ -269,7 +269,7 @@
             own = normed[:, 0:LANES]
             for j in range(1, m):
                 own = jnp.where(mp == j, normed[:, j * LANES : (j + 1) * LANES], own)
-            d_points[r, :] = own
+            normq[r, :] = own
             proj = dotf(hidden, wcat)
             q, k, val = (proj[:, t * LANES : (t + 1) * LANES].astype(BF) for t in range(3))
             kn[r, :] = k
@@ -318,18 +318,32 @@
         normalise(p)
         scores(p, 0, 0)
 
-        def step(h, _):
-            @pl.when(lax.rem(h, 2) == 0)
-            def _():
-                relay(dout, 1, p * PBLK + h // 2)
-
-            scores(p, h, 1)
-            forward(p, h, 0)
-            scores(p, jnp.minimum(h + 1, HEADS - 1), 0)
-            forward(p, h, 1)
+        def step(i, _):
+            h = i // 2
+
+            b = (p * 2 * HEADS + i - HEADS) // 2
+
+            @pl.when(jnp.logical_and(lax.rem(i, 2) == 0, jnp.logical_and(b >= 0, b < blocks)))
+            def _():
+                relay(dout, 1, b)
+
+            @pl.when(lax.rem(i, 2) == 0)
+            def _():
+                scores(p, h, 1)
+                forward(p, h, 0)
+
+            @pl.when(jnp.logical_and(lax.rem(i, 2) == 1, h < HEADS - 1))
+            def _():
+                scores(p, h + 1, 0)
+                forward(p, h, 1)
+
+            @pl.when(i == 2 * HEADS - 1)
+            def _():
+                forward(p, HEADS - 1, 1)
+
             return 0
 
-        lax.fori_loop(0, HEADS, step, 0)
+        lax.fori_loop(0, 2 * HEADS, step, 0)
         return 0
 
     lax.fori_loop(0, npatch, forward_patch, 0)
@@ -420,7 +434,7 @@
             for j in range(m):
                 part[j, r, :] = pd[:, j * LANES : (j + 1) * LANES]
             if b % 2 == 1:
-                for c in hops(p, *((0, 3), (1, 2))[b // 2]):
+                for c in hops(p, *((0,), (1, 3, 2))[b // 2]):
                     c.start()
             gram = dot_nt(pd, hid[r, :])
             cross = jnp.sum(jnp.where(iota((BLK, BLK), 0) == iota((BLK, BLK), 1), gram, 0.0), axis=0, keepdims=True)
@@ -466,9 +480,12 @@
             mean_grad = lane_copy(st[2 * b : 2 * b + 1])
             mean_cross = lane_copy(st[2 * b + 1 : 2 * b + 2])
             d_hidden = part[mp, r, :].astype(F32) + got_l[r, :].astype(F32) + got_r[r, :].astype(F32)
-            d_points[r, :] = dout[mp, r, :].astype(F32) + invb[r, :] * (
-                d_hidden - mean_grad - d_points[r, :] * mean_cross
+            grad = dout[mp, r, :].astype(F32) + invb[r, :] * (
+                d_hidden - mean_grad - normq[r, :] * mean_cross
             )
+            high = grad.astype(BF)
+            d_high[r, :] = high
+            d_low[r, :] = (grad - high.astype(F32)).astype(BF)
 
     finish(0)
     others = got_g.at[pl.ds(0, n - 1)]
@@ -500,18 +517,19 @@
     coded = pltpu.VMEM((n, 16, cap), BF)
     full = pltpu.VMEM((m, rows, LANES), BF)
     hop_buf = pltpu.VMEM((npatch, PATCH // 2, LANES), BF)
-    d_points, grad_qkv, grad_out = (
+    d_high, d_low, grad_qkv, grad_out = (
         pl.pallas_call(
             layer_kernel,
             out_shape=[
-                jax.ShapeDtypeStruct((rows, LANES), F32),
+                jax.ShapeDtypeStruct((rows, LANES), BF),
+                jax.ShapeDtypeStruct((rows, LANES), BF),
                 jax.ShapeDtypeStruct((3, band, LANES), F32),
                 jax.ShapeDtypeStruct((band, LANES), F32),
             ],
             in_specs=[hbm, hbm] + [vmem] * 6,
-            out_specs=[vmem] * 3,
+            out_specs=[vmem] * 4,
             scratch_shapes=[
-                col, col, col, pltpu.VMEM((n * cap, LANES), BF), coded,
+                pltpu.VMEM((rows, LANES), F32), col, col, col, pltpu.VMEM((n * cap, LANES), BF), coded,
                 col, pltpu.VMEM((n * cap, LANES), BF), coded, pltpu.VMEM((blocks, BLK), jnp.int32), pltpu.VMEM((n, cap), F32),
                 full, full, pltpu.VMEM((rows, feats), BF), col, col,
                 pltpu.VMEM((npatch, 2 * LANES, PATCH), BF),
@@ -541,7 +559,7 @@
             voxel_shard.reshape(1, -1), jnp.transpose(qkv_weight, (1, 0, 2)), out_weight,
         )
     )
-    return d_points, jnp.transpose(grad_qkv, (1, 0, 2)), grad_out
+    return d_high.astype(F32) + d_low.astype(F32), jnp.transpose(grad_qkv, (1, 0, 2)), grad_out
 
 
 def solution(mesh):

time: 119 us -> 118 us (level)
  local copies, waits for them, and re-layouts: 3.49 us -> 1.21 us
  other arithmetic: 0 us -> 2.28 us
    add x0 -> x1, other arithmetic: none -> 2.28 us  [local(): d_high.astype(F32) + d_low.astype(F32)]
    unnamed x7 -> x6, local copies, waits for them, and re-layouts: 3.49 us -> 1.21 us
    pallas_call x1, Pallas kernels: 115 us -> 114 us  [local(): pl.pallas_call(layer_kernel, out_shape=[jax.ShapeDtypeStruct((rows, LANES...]
where the time goes in v5:
time: 118 us
  Pallas kernels  114 us (97%)
  other arithmetic  2.28 us (2%)
  local copies, waits for them, and re-layouts  1.21 us (1%)
    pallas_call x1, Pallas kernels, local(): pl.pallas_call(layer_kernel, out_shape=[jax.ShapeDtypeStruct((rows, LANES...  114 us

profile of v5, /device:TPU:1, one launch (start us, length us, event | category | flops | bytes accessed | tf_op | source)
XLA Modules:
  0.0 117.7 jit_solution(12723487279105069118)
XLA Ops:
  0.6 113.5 %layer.1 = (bf16[2048,128]{1,0:T(8,128)(2,1)}, bf16[2048,128]{1,0:T(8,128)(2,1)}, f32[3,16,128]{2,1,0:T(8,128)}, f32[16,128]{1,0:T(8,128)}) custom-call(bf16[2048,512]{1,0:T(8,128)(2,1)} %scan.1, bf16[2048,512]{1,0:T(8,128)(2,1)} %voxels.1, s32[16,128]{1,0:T(8,128)} %bitcast.8, s32[16,128]{1,0:T(8,128)} %bitcast.9, s32[16,128]{1,0:T(8,128)} %bitcast.10, ...), custom_call_target="tpu_custom_call" | custom-call | tf_op jit(solution)/shard_map/layer/pallas_call | solution.py:521
  114.2 0.0 copy-start
  114.2 0.0 copy-start.1
  114.2 2.3 %convert_add_fusion = f32[2048,128]{1,0:T(8,128)} fusion(bf16[2048,128]{1,0:T(8,128)(2,1)} %get-tuple-element.8, bf16[2048,128]{1,0:T(8,128)(2,1)} %get-tuple-element.7), kind=kLoop, calls=%fused_computation | loop fusion | flops 786432 | bytes 2097152 | tf_op jit(solution)/shard_map/add | solution.py:562
  116.5 0.0 copy-done
  116.5 0.6 copy.13
  117.1 0.0 copy-done.1
  117.1 0.6 copy.14
Async XLA Ops:
  114.2 2.3 %copy-start = (f32[3,16,128]{2,1,0:T(8,128)S(1)}, f32[3,16,128]{2,1,0:T(8,128)}, u32[]{:S(2)}) copy-start(f32[3,16,128]{2,1,0:T(8,128)} %get-tuple-element.9) | copy-start | bytes 73732
  114.2 2.9 %copy-start.1 = (f32[16,128]{1,0:T(8,128)S(1)}, f32[16,128]{1,0:T(8,128)}, u32[]{:S(2)}) copy-start(f32[16,128]{1,0:T(8,128)} %get-tuple-element.16) | copy-start | bytes 24580

commit v6 on v5

--- a/solution.py
+++ b/solution.py
@@ -183,9 +183,7 @@
 
         return 0
 
-    lax.fori_loop(0, vblocks, voxels_out, 0)
-    gotv[rows_of(seq, cap), :] = sendv[rows_of(seq, cap), :]
-    goti[seq] = sendi[seq]
+    lax.fori_loop(0, vblocks // 2, voxels_out, 0)
 
     def wait_all(kind, ref, size):
         other = ref.at[pl.ds(0, size)]
@@ -235,6 +233,9 @@
         return 0
 
     lax.fori_loop(0, blocks, points_in, 0)
+    lax.fori_loop(vblocks // 2, vblocks, voxels_out, 0)
+    gotv[rows_of(seq, cap), :] = sendv[rows_of(seq, cap), :]
+    goti[seq] = sendi[seq]
     wait_all(1, gotv, (n - 1) * cap)
     wait_all(2, goti, n - 1)
     for t in range(n):
@@ -321,7 +322,7 @@
         def step(i, _):
             h = i // 2
 
-            b = (p * 2 * HEADS + i - HEADS) // 2
+            b = (p * 2 * HEADS + i - 6) // 2
 
             @pl.when(jnp.logical_and(lax.rem(i, 2) == 0, jnp.logical_and(b >= 0, b < blocks)))
             def _():

time: 118 us -> 123 us (1.042)
  Pallas kernels: 114 us -> 119 us
    pallas_call x1, Pallas kernels: 114 us -> 119 us  [local(): pl.pallas_call(layer_kernel, out_shape=[jax.ShapeDtypeStruct((rows, LANES...]
where the time goes in v6:
time: 123 us
  Pallas kernels  119 us (97%)
  other arithmetic  2.28 us (2%)
    pallas_call x1, Pallas kernels, local(): pl.pallas_call(layer_kernel, out_shape=[jax.ShapeDtypeStruct((rows, LANES...  119 us

profile of v6, /device:TPU:1, one launch (start us, length us, event | category | flops | bytes accessed | tf_op | source)
XLA Modules:
  0.0 122.7 jit_solution(5770804426582209056)
XLA Ops:
  0.6 118.5 %layer.1 = (bf16[2048,128]{1,0:T(8,128)(2,1)}, bf16[2048,128]{1,0:T(8,128)(2,1)}, f32[3,16,128]{2,1,0:T(8,128)}, f32[16,128]{1,0:T(8,128)}) custom-call(bf16[2048,512]{1,0:T(8,128)(2,1)} %scan.1, bf16[2048,512]{1,0:T(8,128)(2,1)} %voxels.1, s32[16,128]{1,0:T(8,128)} %bitcast.8, s32[16,128]{1,0:T(8,128)} %bitcast.9, s32[16,128]{1,0:T(8,128)} %bitcast.10, ...), custom_call_target="tpu_custom_call" | custom-call | tf_op jit(solution)/shard_map/layer/pallas_call | solution.py:522
  119.1 0.0 copy-start
  119.2 0.0 copy-start.1
  119.2 2.3 %convert_add_fusion = f32[2048,128]{1,0:T(8,128)} fusion(bf16[2048,128]{1,0:T(8,128)(2,1)} %get-tuple-element.8, bf16[2048,128]{1,0:T(8,128)(2,1)} %get-tuple-element.7), kind=kLoop, calls=%fused_computation | loop fusion | flops 786432 | bytes 2097152 | tf_op jit(solution)/shard_map/add | solution.py:563
  121.4 0.0 copy-done
  121.5 0.6 copy.13
  122.1 0.0 copy-done.1
  122.1 0.6 copy.14
Async XLA Ops:
  119.1 2.3 %copy-start = (f32[3,16,128]{2,1,0:T(8,128)S(1)}, f32[3,16,128]{2,1,0:T(8,128)}, u32[]{:S(2)}) copy-start(f32[3,16,128]{2,1,0:T(8,128)} %get-tuple-element.9) | copy-start | bytes 73732
  119.2 2.9 %copy-start.1 = (f32[16,128]{1,0:T(8,128)S(1)}, f32[16,128]{1,0:T(8,128)}, u32[]{:S(2)}) copy-start(f32[16,128]{1,0:T(8,128)} %get-tuple-element.16) | copy-start | bytes 24580

commit v7 on v5

--- a/solution.py
+++ b/solution.py
@@ -82,7 +82,7 @@
 
 def layer_kernel(
     scan, voxels, send_order, arrive_order, point, shard, w, wo,
-    d_high, d_low, grad_qkv, grad_out,
+    d_high, d_low, grad_all,
     normq, x, v, sendp, sendv, sendi, gotp, gotv, goti, place, at_all,
     pts, dout, hid, kn, vn, qhl, qt, kt, vt, dat, dpt, qm0, qm1, s0, s1, e_all, ds0, ds1, top, linv, dst, est,
     grads, stats, invb, rel_l, rel_r, got_s, got_g,
@@ -436,6 +436,9 @@
             if b % 2 == 1:
                 for c in hops(p, *((0,), (1, 3, 2))[b // 2]):
                     c.start()
+        for b in range(PBLK):
+            r = rows_of(p * PBLK + b, BLK)
+            pd = lanes_of(part, r)
             gram = dot_nt(pd, hid[r, :])
             cross = jnp.sum(jnp.where(iota((BLK, BLK), 0) == iota((BLK, BLK), 1), gram, 0.0), axis=0, keepdims=True)
             total = dot_nt(jnp.ones((8, pd.shape[1]), BF), pd)
@@ -493,9 +496,8 @@
     total = jnp.zeros((band, grads.shape[1]), F32)
     for k in range(n):
         total = total + got_g[k].astype(F32)
-    for t in range(3):
-        grad_qkv[t] = total[:, t * LANES : (t + 1) * LANES]
-    grad_out[...] = total[:, 3 * LANES : 4 * LANES]
+    for t in range(4):
+        grad_all[t] = total[:, t * LANES : (t + 1) * LANES]
     finish(1)
 
 
@@ -517,17 +519,16 @@
     coded = pltpu.VMEM((n, 16, cap), BF)
     full = pltpu.VMEM((m, rows, LANES), BF)
     hop_buf = pltpu.VMEM((npatch, PATCH // 2, LANES), BF)
-    d_high, d_low, grad_qkv, grad_out = (
+    d_high, d_low, grad_all = (
         pl.pallas_call(
             layer_kernel,
             out_shape=[
                 jax.ShapeDtypeStruct((rows, LANES), BF),
                 jax.ShapeDtypeStruct((rows, LANES), BF),
-                jax.ShapeDtypeStruct((3, band, LANES), F32),
-                jax.ShapeDtypeStruct((band, LANES), F32),
+                jax.ShapeDtypeStruct((4, band, LANES), F32),
             ],
             in_specs=[hbm, hbm] + [vmem] * 6,
-            out_specs=[vmem] * 4,
+            out_specs=[vmem] * 3,
             scratch_shapes=[
                 pltpu.VMEM((rows, LANES), F32), col, col, col, pltpu.VMEM((n * cap, LANES), BF), coded,
                 col, pltpu.VMEM((n * cap, LANES), BF), coded, pltpu.VMEM((blocks, BLK), jnp.int32), pltpu.VMEM((n, cap), F32),
@@ -559,7 +560,7 @@
             voxel_shard.reshape(1, -1), jnp.transpose(qkv_weight, (1, 0, 2)), out_weight,
         )
     )
-    return d_high.astype(F32) + d_low.astype(F32), jnp.transpose(grad_qkv, (1, 0, 2)), grad_out
+    return d_high.astype(F32) + d_low.astype(F32), jnp.transpose(grad_all[:3], (1, 0, 2)), grad_all[3]
 
 
 def solution(mesh):

time: 118 us -> 117 us (level)
    unnamed x6 -> x2, local copies, waits for them, and re-layouts: 1.21 us -> 0.01 us
where the time goes in v7:
time: 117 us
  Pallas kernels  113 us (97%)
  other arithmetic  2.28 us (2%)
  local copies, waits for them, and re-layouts  1.21 us (1%)
    pallas_call x1, Pallas kernels, local(): pl.pallas_call(layer_kernel, out_shape=[jax.ShapeDtypeStruct((rows, LANES...  113 us

profile of v7, /device:TPU:1, one launch (start us, length us, event | category | flops | bytes accessed | tf_op | source)
XLA Modules:
  0.0 117.3 jit_solution(11342997144770811981)
XLA Ops:
  0.6 113.1 %layer.1 = (bf16[2048,128]{1,0:T(8,128)(2,1)}, bf16[2048,128]{1,0:T(8,128)(2,1)}, f32[4,16,128]{2,1,0:T(8,128)}) custom-call(bf16[2048,512]{1,0:T(8,128)(2,1)} %scan.1, bf16[2048,512]{1,0:T(8,128)(2,1)} %voxels.1, s32[16,128]{1,0:T(8,128)} %bitcast.10, s32[16,128]{1,0:T(8,128)} %bitcast.11, s32[16,128]{1,0:T(8,128)} %bitcast.12, s32[1,2048]{1,0:T(1,128)} %bitcast.13, ...), custom_call_target="tpu_custom_call" | custom-call | tf_op jit(solution)/shard_map/layer/pallas_call | solution.py:523
  113.8 0.0 copy-start
  113.8 2.3 %convert_add_fusion = f32[2048,128]{1,0:T(8,128)} fusion(bf16[2048,128]{1,0:T(8,128)(2,1)} %get-tuple-element.7, bf16[2048,128]{1,0:T(8,128)(2,1)} %get-tuple-element.6), kind=kLoop, calls=%fused_computation | loop fusion | flops 786432 | bytes 2097152 | tf_op jit(solution)/shard_map/add | solution.py:563
  116.1 0.0 copy-done
  116.1 0.6 slice_bitcast_fusion.1
  116.7 0.6 slice_bitcast_fusion
Async XLA Ops:
  113.8 2.3 %copy-start = (f32[4,16,128]{2,1,0:T(8,128)S(1)}, f32[4,16,128]{2,1,0:T(8,128)}, u32[]{:S(2)}) copy-start(f32[4,16,128]{2,1,0:T(8,128)} %get-tuple-element.8) | copy-start | bytes 98308

commit v8 on v7

--- a/solution.py
+++ b/solution.py
@@ -321,7 +321,7 @@
         def step(i, _):
             h = i // 2
 
-            b = (p * 2 * HEADS + i - HEADS) // 2
+            b = (p * 2 * HEADS + i - HEADS - 2) // 2
 
             @pl.when(jnp.logical_and(lax.rem(i, 2) == 0, jnp.logical_and(b >= 0, b < blocks)))
             def _():
@@ -473,12 +473,13 @@
     scale = 1.0 / (m * LANES)
 
     def finish(p):
-        for c in hops(p, 2, 3, 4, 5):
-            c.wait()
         for i, to in enumerate((right, left, opposite)):
             stat_copy(p, i, to).wait()
         st = (stats[p] + got_s[p, 0] + got_s[p, 1] + got_s[p, 2]) * scale
         for b in range(PBLK):
+            if b % 2 == 0:
+                for c in hops(p, *((3, 4), (2, 5))[b // 2]):
+                    c.wait()
             r = pl.ds(p * PATCH + b * BLK, BLK)
             mean_grad = lane_copy(st[2 * b : 2 * b + 1])
             mean_cross = lane_copy(st[2 * b + 1 : 2 * b + 2])

time: 117 us -> 117 us (level)
  no operation moved by 1% of the time
where the time goes in v8:
time: 117 us
  Pallas kernels  113 us (97%)
  other arithmetic  2.28 us (2%)
  local copies, waits for them, and re-layouts  1.21 us (1%)
    pallas_call x1, Pallas kernels, local(): pl.pallas_call(layer_kernel, out_shape=[jax.ShapeDtypeStruct((rows, LANES...  113 us

profile of v8, /device:TPU:1, one launch (start us, length us, event | category | flops | bytes accessed | tf_op | source)
XLA Modules:
  0.0 117.3 jit_solution(9049616207706521895)
XLA Ops:
  0.6 113.2 %layer.1 = (bf16[2048,128]{1,0:T(8,128)(2,1)}, bf16[2048,128]{1,0:T(8,128)(2,1)}, f32[4,16,128]{2,1,0:T(8,128)}) custom-call(bf16[2048,512]{1,0:T(8,128)(2,1)} %scan.1, bf16[2048,512]{1,0:T(8,128)(2,1)} %voxels.1, s32[16,128]{1,0:T(8,128)} %bitcast.10, s32[16,128]{1,0:T(8,128)} %bitcast.11, s32[16,128]{1,0:T(8,128)} %bitcast.12, s32[1,2048]{1,0:T(1,128)} %bitcast.13, ...), custom_call_target="tpu_custom_call" | custom-call | tf_op jit(solution)/shard_map/layer/pallas_call | solution.py:524
  113.8 0.0 copy-start
  113.8 2.3 %convert_add_fusion = f32[2048,128]{1,0:T(8,128)} fusion(bf16[2048,128]{1,0:T(8,128)(2,1)} %get-tuple-element.7, bf16[2048,128]{1,0:T(8,128)(2,1)} %get-tuple-element.6), kind=kLoop, calls=%fused_computation | loop fusion | flops 786432 | bytes 2097152 | tf_op jit(solution)/shard_map/add | solution.py:564
  116.1 0.0 copy-done
  116.1 0.6 slice_bitcast_fusion.1
  116.7 0.6 slice_bitcast_fusion
Async XLA Ops:
  113.8 2.3 %copy-start = (f32[4,16,128]{2,1,0:T(8,128)S(1)}, f32[4,16,128]{2,1,0:T(8,128)}, u32[]{:S(2)}) copy-start(f32[4,16,128]{2,1,0:T(8,128)} %get-tuple-element.8) | copy-start | bytes 98308

commit v9 on v8

--- a/solution.py
+++ b/solution.py
@@ -321,7 +321,7 @@
         def step(i, _):
             h = i // 2
 
-            b = (p * 2 * HEADS + i - HEADS - 2) // 2
+            b = (p * 2 * HEADS + i - HEADS - 4) // 2
 
             @pl.when(jnp.logical_and(lax.rem(i, 2) == 0, jnp.logical_and(b >= 0, b < blocks)))
             def _():

time: 117 us -> 118 us (level)
  no operation moved by 1% of the time
where the time goes in v9:
time: 118 us; the launch traced here: 117 us
  Pallas kernels  113 us (96%)
  other arithmetic  2.28 us (2%)
  local copies, waits for them, and re-layouts  1.21 us (1%)
    pallas_call x1, Pallas kernels, local(): pl.pallas_call(layer_kernel, out_shape=[jax.ShapeDtypeStruct((rows, LANES...  113 us

profile of v9, /device:TPU:1, one launch (start us, length us, event | category | flops | bytes accessed | tf_op | source)
XLA Modules:
  0.0 117.4 jit_solution(9838794178371821043)
XLA Ops:
  0.6 113.2 %layer.1 = (bf16[2048,128]{1,0:T(8,128)(2,1)}, bf16[2048,128]{1,0:T(8,128)(2,1)}, f32[4,16,128]{2,1,0:T(8,128)}) custom-call(bf16[2048,512]{1,0:T(8,128)(2,1)} %scan.1, bf16[2048,512]{1,0:T(8,128)(2,1)} %voxels.1, s32[16,128]{1,0:T(8,128)} %bitcast.10, s32[16,128]{1,0:T(8,128)} %bitcast.11, s32[16,128]{1,0:T(8,128)} %bitcast.12, s32[1,2048]{1,0:T(1,128)} %bitcast.13, ...), custom_call_target="tpu_custom_call" | custom-call | tf_op jit(solution)/shard_map/layer/pallas_call | solution.py:524
  113.9 0.0 copy-start
  113.9 2.3 %convert_add_fusion = f32[2048,128]{1,0:T(8,128)} fusion(bf16[2048,128]{1,0:T(8,128)(2,1)} %get-tuple-element.7, bf16[2048,128]{1,0:T(8,128)(2,1)} %get-tuple-element.6), kind=kLoop, calls=%fused_computation | loop fusion | flops 786432 | bytes 2097152 | tf_op jit(solution)/shard_map/add | solution.py:564
  116.1 0.0 copy-done
  116.2 0.6 slice_bitcast_fusion.1
  116.8 0.6 slice_bitcast_fusion
Async XLA Ops:
  113.9 2.3 %copy-start = (f32[4,16,128]{2,1,0:T(8,128)S(1)}, f32[4,16,128]{2,1,0:T(8,128)}, u32[]{:S(2)}) copy-start(f32[4,16,128]{2,1,0:T(8,128)} %get-tuple-element.8) | copy-start | bytes 98308
